TPU v7x, 32 devices: a whole 2x2x4 slice. The times are simulated.
32 devices in a mesh: dp: 8 (over z, x), mp: 4 (over y, core).
Axes of the slice: x: 2, y: 2, z: 4, core: 2. Of those that a mesh axis runs over, the one named last changes fastest.
Arguments:
- tokens: bfloat16 [18944, 768], P(('dp', 'mp')), may hold values from -6 to 6
- image_group: int32 [8], P('dp'), may hold values from 0 to 1, as said below
- positions: int32 [2, 18944], P(None, 'dp'), may hold values from 0 to 23, as said below
- keep_mask: int32 [18944], P('dp'), may hold values from 0 to 1, as said below
- norm1_gain: float32 [768], replicated, may hold values from 0.25 to 1.75
- norm1_bias: float32 [768], replicated, may hold values from -1.75 to 1.75
- w_qkv: bfloat16 [768, 3, 768], P(None, None, 'mp'), may hold values from -0.21875 to 0.21875
- b_qkv: float32 [3, 768], P(None, 'mp'), may hold values from -1.75 to 1.75
- rotary_freqs: float32 [2, 12, 32], P(None, 'mp'), may hold values from -1 to 1
- w_out: bfloat16 [768, 768], P('mp'), may hold values from -0.875 to 0.875
- b_out: float32 [768], replicated, may hold values from -1.75 to 1.75
- norm2_gain: float32 [768], replicated, may hold values from 0.25 to 1.75
- norm2_bias: float32 [768], replicated, may hold values from -1.75 to 1.75
- w_up: bfloat16 [768, 3072], P(None, 'mp'), may hold values from -0.21875 to 0.21875
- b_up: bfloat16 [3072], P('mp'), may hold values from -1.75 to 1.75
- w_down: bfloat16 [3072, 768], P('mp'), may hold values from -0.109375 to 0.109375
- b_down: float32 [768], replicated, may hold values from -1.75 to 1.75
- cotangent: float32 [18944, 768], P(('dp', 'mp')), may hold values from -6 to 6
Outputs:
- output: bfloat16 [18944, 768], P(('dp', 'mp'))
- grad_tokens: float32 [18944, 768], P(('dp', 'mp'))
- grad_norm1_gain: float32 [768], replicated
- grad_norm1_bias: float32 [768], replicated
- grad_w_qkv: float32 [768, 3, 768], P(None, None, 'mp')
- grad_b_qkv: float32 [3, 768], P(None, 'mp')
- grad_rotary_freqs: float32 [2, 12, 32], P(None, 'mp')
- grad_w_out: float32 [768, 768], P('mp')
- grad_b_out: float32 [768], replicated
- grad_norm2_gain: float32 [768], replicated
- grad_norm2_bias: float32 [768], replicated
- grad_w_up: float32 [768, 3072], P(None, 'mp')
- grad_b_up: float32 [3072], P('mp')
- grad_w_down: float32 [3072, 768], P('mp')
- grad_b_down: float32 [768], replicated
Inputs may be any that keep to these rules, and one draw needn't show every extreme that they name: `image_group`: exactly 4 entries are 1. `positions`: each image's slots carry each of its patches once; padding slots carry 0, 0. `keep_mask`: in each image the kept slots are its first ones, at least one; padding slots are 0.
All inputs are finite; a program needn't handle non-finite values.
Results may differ from a plain program's by a relative error of at most 0.012.
The roundings to bfloat16 on the way count: a program that leaves them out, or rounds other values in their place, can miss the bound.
Values may be sent and summed in bfloat16 or wider, within the bound.
A program may use at most 192 MiB of HBM per device.

v0:
```python
import math

import jax
import jax.numpy as jnp
from jax import lax
from jax.sharding import PartitionSpec as P

HD = 64
SIDE_SMALL = 14
SIDE_LARGE = 24
IMG_SMALL = 3
IMG_LARGE = 1
PACK = 592


NORM_EPS = 1e-06
MASK_FILL = -1e30


def layer_norm(values, norm_gain, norm_bias):
    row_mean = jnp.mean(values, axis=-1, keepdims=True)
    centered = values - row_mean
    variance = jnp.mean(centered * centered, axis=-1, keepdims=True)
    return centered * lax.rsqrt(variance + NORM_EPS) * norm_gain + norm_bias


def rotate(vector, angles):
    half_size = vector.shape[-1] // 2
    first_half = vector[..., :half_size]
    second_half = vector[..., half_size:]
    cosine = jnp.cos(angles)
    sine_part = jnp.sin(angles)
    return jnp.concatenate(
        [
            first_half * cosine - second_half * sine_part,
            second_half * cosine + first_half * sine_part,
        ],
        axis=-1,
    )


def rotary_pair(queries, keys_in, freq_table, rows_f, cols_f):
    angles = (
        rows_f[:, None, None] * freq_table[0][None] + cols_f[:, None, None] * freq_table[1][None]
    )
    return (rotate(queries, angles), rotate(keys_in, angles))


def gelu_exact(values):
    return jax.nn.gelu(values, approximate=False)


def body(
    tokens,
    image_group,
    positions,
    keep_mask,
    norm1_gain,
    norm1_bias,
    w_qkv,
    b_qkv,
    rotary_freqs,
    w_out,
    b_out,
    norm2_gain,
    norm2_bias,
    w_up,
    b_up,
    w_down,
    b_down,
    cotangent,
):
    own_rows = tokens.shape[0]
    model_size = lax.axis_size("mp")
    data_size = lax.axis_size("dp")
    mp_index = lax.axis_index("mp")
    total_rows = own_rows * model_size
    width = tokens.shape[1]
    score_scale = 1.0 / math.sqrt(HD)
    is_large = image_group[0]
    grid_side = jnp.where(is_large == 1, SIDE_LARGE, SIDE_SMALL)
    image_count = jnp.where(is_large == 1, IMG_LARGE, IMG_SMALL)
    keep_all = keep_mask.astype(jnp.float32)
    keep_own = lax.dynamic_slice_in_dim(keep_all, mp_index * own_rows, own_rows)
    rows_all = positions[0].astype(jnp.float32)
    cols_all = positions[1].astype(jnp.float32)
    x_own = tokens.astype(jnp.float32)
    normed_one, norm1_pull = jax.vjp(layer_norm, x_own, norm1_gain, norm1_bias)
    normed_low = normed_one.astype(jnp.bfloat16)
    normed_all = lax.all_gather(normed_low, "mp", axis=0, tiled=True)
    qkv_weight = w_qkv.reshape(width, 3 * w_qkv.shape[2])
    qkv_bias = b_qkv.reshape(3 * b_qkv.shape[1])
    local_width = qkv_weight.shape[1] // 3
    local_heads = rotary_freqs.shape[1]
    pack_count = total_rows // PACK
    inpack = jnp.arange(total_rows, dtype=jnp.int32) % PACK
    image_id = jnp.minimum(inpack // (grid_side * grid_side), image_count - 1).reshape(
        pack_count, PACK
    )
    keep_pack = keep_all.reshape(pack_count, PACK)
    key_valid = (image_id[:, :, None] == image_id[:, None, :]) & (keep_pack[:, None, :] > 0.5)
    projected = jnp.dot(normed_all, qkv_weight, preferred_element_type=jnp.float32) + qkv_bias
    queries = projected[:, :local_width].reshape(total_rows, local_heads, HD)
    keys_raw = projected[:, local_width : 2 * local_width].reshape(total_rows, local_heads, HD)
    value_b = (
        projected[:, 2 * local_width :]
        .astype(jnp.bfloat16)
        .reshape(pack_count, PACK, local_heads, HD)
    )

    def turn_both(query_in, key_in, freq_in):
        return rotary_pair(query_in, key_in, freq_in, rows_all, cols_all)

    (turned_q, turned_k), rotary_pull = jax.vjp(turn_both, queries, keys_raw, rotary_freqs)
    query_b = turned_q.astype(jnp.bfloat16).reshape(pack_count, PACK, local_heads, HD)
    key_b = turned_k.astype(jnp.bfloat16).reshape(pack_count, PACK, local_heads, HD)
    scores = (
        jnp.einsum("pqhd,pkhd->phqk", query_b, key_b, preferred_element_type=jnp.float32)
        * score_scale
    )
    masked = jnp.where(key_valid[:, None], scores, MASK_FILL)
    row_max = jnp.max(masked, axis=-1, keepdims=True)
    exp_terms = jnp.where(key_valid[:, None], jnp.exp(masked - row_max), 0.0)
    row_total = jnp.sum(exp_terms, axis=-1, keepdims=True)
    attn_probs = exp_terms / row_total
    log_total = row_max + jnp.log(row_total)
    attended = jnp.einsum(
        "phqk,pkhd->pqhd",
        attn_probs.astype(jnp.bfloat16),
        value_b,
        preferred_element_type=jnp.float32,
    )
    attended_b = attended.reshape(total_rows, local_width).astype(jnp.bfloat16)
    branch = (
        lax.psum_scatter(
            jnp.dot(attended_b, w_out, preferred_element_type=jnp.float32),
            "mp",
            scatter_dimension=0,
            tiled=True,
        )
        + b_out
    )
    middle = x_own + branch
    normed_two, norm2_pull = jax.vjp(layer_norm, middle, norm2_gain, norm2_bias)
    second_b = normed_two.astype(jnp.bfloat16)
    grad_out = cotangent * keep_own[:, None]
    grad_out_b = grad_out.astype(jnp.bfloat16)
    grad_b_down = jnp.sum(grad_out_b.astype(jnp.float32), axis=0)
    second_all = lax.all_gather(second_b, "mp", axis=0, tiled=True)
    hidden = jnp.dot(second_all, w_up, preferred_element_type=jnp.float32) + b_up.astype(
        jnp.float32
    )
    hidden_act, gelu_pull = jax.vjp(gelu_exact, hidden)
    active_b = hidden_act.astype(jnp.bfloat16)
    mlp_branch = (
        lax.psum_scatter(
            jnp.dot(active_b, w_down, preferred_element_type=jnp.float32).astype(jnp.bfloat16),
            "mp",
            scatter_dimension=0,
            tiled=True,
        ).astype(jnp.float32)
        + b_down
    )
    grad_all = lax.all_gather(grad_out_b, "mp", axis=0, tiled=True)
    grad_w_down = jnp.einsum("tf,td->fd", active_b, grad_all, preferred_element_type=jnp.float32)
    grad_active = jnp.einsum("td,fd->tf", grad_all, w_down, preferred_element_type=jnp.float32)
    grad_hidden_b = gelu_pull(grad_active)[0].astype(jnp.bfloat16)
    grad_w_up = jnp.einsum(
        "td,tf->df", second_all, grad_hidden_b, preferred_element_type=jnp.float32
    )
    grad_b_up = jnp.sum(grad_hidden_b.astype(jnp.float32), axis=0)
    grad_second = lax.psum_scatter(
        jnp.einsum("tf,df->td", grad_hidden_b, w_up, preferred_element_type=jnp.float32),
        "mp",
        scatter_dimension=0,
        tiled=True,
    )
    output = (middle + mlp_branch).astype(jnp.bfloat16)
    grad_mid_norm, grad_gain2, grad_bias2 = norm2_pull(grad_second)
    grad_middle = grad_out + grad_mid_norm
    branch_grad_b = grad_middle.astype(jnp.bfloat16)
    grad_b_out = jnp.sum(branch_grad_b.astype(jnp.float32), axis=0)
    branch_all = lax.all_gather(branch_grad_b, "mp", axis=0, tiled=True)
    grad_w_out = jnp.einsum("tc,td->cd", attended_b, branch_all, preferred_element_type=jnp.float32)
    grad_att_b = (
        jnp.einsum("td,cd->tc", branch_all, w_out, preferred_element_type=jnp.float32)
        .astype(jnp.bfloat16)
        .reshape(pack_count, PACK, local_heads, HD)
    )
    again = (
        jnp.einsum("pqhd,pkhd->phqk", query_b, key_b, preferred_element_type=jnp.float32)
        * score_scale
    )
    again_masked = jnp.where(key_valid[:, None], again, MASK_FILL)
    probs_again = jnp.where(key_valid[:, None], jnp.exp(again_masked - log_total), 0.0)
    grad_probs = jnp.einsum(
        "pqhd,pkhd->phqk", grad_att_b, value_b, preferred_element_type=jnp.float32
    )
    grad_value = jnp.einsum(
        "phqk,pqhd->pkhd",
        probs_again.astype(jnp.bfloat16),
        grad_att_b,
        preferred_element_type=jnp.float32,
    )
    inner_sum = jnp.sum(probs_again * grad_probs, axis=-1, keepdims=True)
    grad_scores_b = (probs_again * (grad_probs - inner_sum)).astype(jnp.bfloat16)
    grad_query = (
        jnp.einsum("phqk,pkhd->pqhd", grad_scores_b, key_b, preferred_element_type=jnp.float32)
        * score_scale
    )
    grad_key = (
        jnp.einsum("phqk,pqhd->pkhd", grad_scores_b, query_b, preferred_element_type=jnp.float32)
        * score_scale
    )
    grad_q_raw, grad_k_raw, grad_freqs = rotary_pull(
        (
            grad_query.reshape(total_rows, local_heads, HD),
            grad_key.reshape(total_rows, local_heads, HD),
        )
    )
    grad_qkv_b = jnp.concatenate(
        [
            grad_q_raw.reshape(total_rows, local_width),
            grad_k_raw.reshape(total_rows, local_width),
            grad_value.reshape(total_rows, local_width),
        ],
        axis=1,
    ).astype(jnp.bfloat16)
    grad_w_qkv = jnp.einsum(
        "td,tc->dc", normed_all, grad_qkv_b, preferred_element_type=jnp.float32
    ).reshape(width, 3, local_width)
    grad_b_qkv = jnp.sum(grad_qkv_b.astype(jnp.float32), axis=0).reshape(3, local_width)
    grad_first = lax.psum_scatter(
        jnp.einsum("tc,dc->td", grad_qkv_b, qkv_weight, preferred_element_type=jnp.float32),
        "mp",
        scatter_dimension=0,
        tiled=True,
    )
    grad_x_norm, grad_gain1, grad_bias1 = norm1_pull(grad_first)
    grad_tokens = grad_middle + grad_x_norm
    count_own = jnp.sum(keep_own)
    counted = lax.psum(count_own, ("dp", "mp"))
    factor = data_size / counted
    grad_gain1, grad_bias1, grad_b_out, grad_gain2, grad_bias2, grad_b_down = lax.psum(
        (
            grad_gain1 * factor,
            grad_bias1 * factor,
            grad_b_out * factor,
            grad_gain2 * factor,
            grad_bias2 * factor,
            grad_b_down * factor,
        ),
        ("dp", "mp"),
    )
    after_sum = 1.0
    grad_w_qkv, grad_b_qkv, grad_freqs, grad_w_out, grad_w_up, grad_b_up, grad_w_down = lax.psum(
        (
            grad_w_qkv * factor,
            grad_b_qkv * factor,
            grad_freqs * factor,
            grad_w_out * factor,
            grad_w_up * factor,
            grad_b_up * factor,
            grad_w_down * factor,
        ),
        "dp",
    )
    return (
        output,
        grad_tokens,
        grad_gain1,
        grad_bias1,
        grad_w_qkv * after_sum,
        grad_b_qkv * after_sum,
        grad_freqs * after_sum,
        grad_w_out * after_sum,
        grad_b_out,
        grad_gain2,
        grad_bias2,
        grad_w_up * after_sum,
        grad_b_up * after_sum,
        grad_w_down * after_sum,
        grad_b_down,
    )


def solution(mesh):
    placed = (
        P(("dp", "mp"), None),
        P("dp"),
        P(None, "dp"),
        P("dp"),
        P(),
        P(),
        P(None, None, "mp"),
        P(None, "mp"),
        P(None, "mp", None),
        P("mp", None),
        P(),
        P(),
        P(),
        P(None, "mp"),
        P("mp"),
        P("mp", None),
        P(),
        P(("dp", "mp"), None),
    )
    return jax.shard_map(
        body,
        mesh=mesh,
        in_specs=placed,
        out_specs=(
            P(("dp", "mp"), None),
            P(("dp", "mp"), None),
            P(),
            P(),
            P(None, None, "mp"),
            P(None, "mp"),
            P(None, "mp", None),
            P("mp", None),
            P(),
            P(),
            P(),
            P(None, "mp"),
            P("mp"),
            P("mp", None),
            P(),
        ),
        check_vma=False,
    )
```

profile of v0, /device:TPU:0, one launch (start us, length us, event | category | flops | bytes accessed | tf_op | source)
XLA Modules:
  0.0 840.2 jit_solution(1473489827181367015)
XLA Ops:
  8.8 1.6 fusion.20
  11.5 2.5 fusion.18
  16.8 31.5 %all-gather.5.cloned.1.call-done = bf16[2368,768]{1,0:T(8,128)(2,1)} async-done(((bf16[592,768]{1,0:T(8,128)(2,1)}), bf16[2368,768]{1,0:T(8,128)(2,1)}) %all-gather.5.cloned.1.call-update) | async-done | bytes 3637264 | tf_op jit(solution)/shard_map/all_gather | solution.py:90
  48.3 4.8 convolution_add_fusion
  54.0 2.1 fusion.59
  56.1 3.4 reshape.250
  59.5 7.1 add_convert_fusion.5
  66.7 1.6 concatenate.26
  68.2 2.3 concatenate.25
  70.6 1.9 copy_dynamic-update-slice_fusion.1
  72.4 2.3 concatenate.22
  74.8 1.9 copy_dynamic-update-slice_fusion.3
  76.6 2.3 concatenate.23
  79.8 1.9 copy_dynamic-update-slice_fusion.2
  81.7 5.2 fusion.1
  86.8 6.2 copy-done.1
  93.1 5.0 fusion
  98.1 9.9 %fusion.29 = bf16[4,592,3,64]{1,3,2,0:T(8,128)(2,1)S(1)} fusion(f32[4,3,592,592]{2,3,1,0:T(8,128)} %copy-done.1, f32[4,3,592]{2,1,0:T(4,128)S(1)} %fusion, f32[4,3,592]{2,1,0:T(4,128)S(1)} %get-tuple-element.98, pred[4,592,592]{1,2,0:T(8,128)(4,1)S(1)} %compare_and_fusion, bf16[4,592,3,64]{1,0,3,2:T(4,128)(2,1)S(1)} %copy-done.24), kind=kOutput, calls=%fused_computation.72 | convolution fusion | flops 564000768 | bytes 20099584 | tf_op jit(solution)/shard_map/phqk,pkhd->pqhd/dot_general | solution.py:127
  109.5 4.1 fusion.61
  113.8 65.1 %reduce-scatter.5.cloned.1.call-done = f32[592,768]{1,0:T(8,128)} async-done(((f32[2368,768]{1,0:T(8,128)}), f32[592,768]{1,0:T(8,128)}) %reduce-scatter.5.cloned.1.call-update) | async-done | bytes 1818640 | tf_op jit(solution)/shard_map/reduce_scatter | solution.py:135
  178.9 2.0 fusion.58
  183.3 3.2 convert_reduce_fusion.3
  186.7 27.4 %all-gather.7.cloned.1.call-done = bf16[2368,768]{1,0:T(8,128)(2,1)} async-done(((bf16[592,768]{1,0:T(8,128)(2,1)}), bf16[2368,768]{1,0:T(8,128)(2,1)}) %all-gather.7.cloned.1.call-update) | async-done | bytes 3637264 | tf_op jit(solution)/shard_map/all_gather | solution.py:149
  214.1 8.3 fusion.62
  222.4 25.1 %all-gather.9.cloned.1.call-done = bf16[2368,768]{1,0:T(8,128)(2,1)} async-done(((bf16[592,768]{1,0:T(8,128)(2,1)}), bf16[2368,768]{1,0:T(8,128)(2,1)}) %all-gather.9.cloned.1.call-update) | async-done | bytes 3637264 | tf_op jit(solution)/shard_map/all_gather | solution.py:164
  247.5 22.6 %convert_reduce_fusion = (f32[768]{0:T(1024)S(1)}, bf16[2368,768]{1,0:T(8,128)(2,1)S(1)}, f32[2368,768]{1,0:T(8,128)}) fusion(f32[2368,768]{1,0:T(8,128)} %fusion.62, f32[768]{0:T(1024)S(1)} %convert_element_type.107, bf16[2368,768]{1,0:T(8,128)(2,1)} %all-gather.9.cloned.1.call-done, bf16[768,768]{1,0:T(8,128)(2,1)S(1)} %copy-done), kind=kOutput, calls=%fused_computation.13 | convolution fusion | flops 2929802496 | bytes 23009280 | tf_op jit(solution)/shard_map/td,fd->tf/dot_general | solution.py:166
  270.1 1.9 copy-done.56
  272.0 5.1 fusion.63
  277.2 6.2 multiply_convert_fusion.1
  283.4 1.8 copy-done.19
  285.2 4.4 convolution_convert_fusion
  289.7 52.7 %reduce-scatter.9.cloned.1.call-done = f32[592,768]{1,0:T(8,128)} async-done(((f32[2368,768]{1,0:T(8,128)}), f32[592,768]{1,0:T(8,128)}) %reduce-scatter.9.cloned.1.call-update) | async-done | bytes 1818640 | tf_op jit(solution)/shard_map/reduce_scatter | solution.py:172
  342.3 2.2 multiply_reduce_fusion.1
  344.5 41.3 %reduce-scatter.7.cloned.1.call-done = bf16[592,768]{1,0:T(8,128)(2,1)} async-done(((bf16[2368,768]{1,0:T(8,128)(2,1)}), bf16[592,768]{1,0:T(8,128)(2,1)}) %reduce-scatter.7.cloned.1.call-update) | async-done | bytes 909328 | tf_op jit(solution)/shard_map/reduce_scatter | solution.py:156
  385.8 3.6 fusion.57
  392.0 31.4 %all-gather.11.cloned.1.call-done = bf16[2368,768]{1,0:T(8,128)(2,1)} async-done(((bf16[592,768]{1,0:T(8,128)(2,1)}), bf16[2368,768]{1,0:T(8,128)(2,1)}) %all-gather.11.cloned.1.call-update) | async-done | bytes 3637264 | tf_op jit(solution)/shard_map/all_gather | solution.py:183
  423.4 4.3 convolution_convert_fusion.1
  427.8 3.5 reshape.253
  431.3 12.0 %fusion.26 = bf16[4,592,3,64]{1,3,2,0:T(8,128)(2,1)S(1)} fusion(f32[4,3,592]{2,1,0:T(4,128)S(1)} %log_add_fusion, f32[4,3,592,592]{2,3,1,0:T(8,128)} %copy-done.1, pred[4,592,592]{1,2,0:T(8,128)(4,1)S(1)} %copy-done.4, bf16[4,592,3,64]{1,0,3,2:T(4,128)(2,1)} %reshape.253), kind=kOutput, calls=%fused_computation.71 | convolution fusion | flops 559795200 | bytes 20071168 | tf_op jit(solution)/shard_map/phqk,pqhd->pkhd/dot_general | solution.py:199
  443.3 19.4 %multiply_reduce_fusion = (f32[4,3,592]{2,1,0:T(4,128)S(1)}, f32[4,3,592,592]{2,3,1,0:T(8,128)}) fusion(f32[4,3,592]{2,1,0:T(4,128)S(1)} %log_add_fusion, f32[4,3,592,592]{2,3,1,0:T(8,128)} %copy-done.1, pred[4,592,592]{1,2,0:T(8,128)(4,1)S(1)} %copy-done.4, bf16[4,592,3,64]{1,0,3,2:T(4,128)(2,1)} %reshape.250, bf16[4,592,3,64]{1,0,3,2:T(4,128)(2,1)} %reshape.253), kind=kOutput, calls=%fused_computation.1 | convolution fusion | flops 563539008 | bytes 36921856 | tf_op jit(solution)/shard_map/pqhd,pkhd->phqk/dot_general | solution.py:196
  462.7 13.4 %multiply_convert_fusion = bf16[4,3,592,592]{2,3,1,0:T(8,128)(2,1)S(1)} fusion(f32[4,3,592,592]{2,3,1,0:T(8,128)} %get-tuple-element.101, f32[4,3,592]{2,1,0:T(4,128)S(1)} %get-tuple-element.100, f32[4,3,592]{2,1,0:T(4,128)S(1)} %log_add_fusion, f32[4,3,592,592]{2,3,1,0:T(8,128)} %copy-done.1, pred[4,592,592]{1,2,0:T(8,128)(4,1)S(1)} %copy-done.4), kind=kLoop, calls=%fused_computation | loop fusion | flops 29438976 | bytes 43514368 | tf_op jit(solution)/shard_map/convert_element_type | solution.py:206
  476.2 4.1 multiply_bitcast_fusion
  480.2 1.7 multiply_bitcast_fusion.1
  481.9 1.7 copy.57
  483.6 2.7 reshape.258
  486.3 2.5 copy.52
  488.8 3.1 reshape.254
  492.0 4.2 copy.54
  496.2 3.1 reshape.256
  499.4 7.2 multiply_add_fusion
  506.6 3.7 multiply_reduce_fusion.5
  512.4 6.0 fusion.51
  518.4 40.0 %psum.98 = f32[]{:T(128)} all-reduce(f32[]{:T(128)} %get-tuple-element.76), channel_id=1, replica_groups=mesh['dp'=8,'mp'=4] {'dp','mp'}, use_global_device_ids=true, to_apply=%region_17.18 | all-reduce | flops 1 | bytes 8 | tf_op jit(solution)/shard_map/psum | solution.py:242
  559.2 8.0 convolution_multiply_fusion.1
  567.2 4.8 convolution_multiply_fusion
  572.0 1.8 convolution_multiply_fusion.3
  573.8 3.7 convolution_multiply_fusion.2
  578.1 1.9 convert_reduce_fusion.1
  580.2 38.1 %all-reduce.7 = (f32[3,192]{1,0:T(4,128)}, f32[2,3,32]{2,1,0:T(4,128)S(1)}, f32[768]{0:T(1024)}) all-reduce(f32[3,192]{1,0:T(4,128)S(1)} %mul.448, f32[2,3,32]{2,1,0:T(4,128)S(1)} %add_multiply_fusion, f32[768]{0:T(1024)S(1)} %broadcast_multiply_fusion.2), channel_id=1, replica_groups=mesh['dp'=8,'mp'=4] {'dp'}, use_global_device_ids=true, to_apply=%region_23.24 | all-reduce | flops 1536 | bytes 12288 | tf_op jit(solution)/shard_map/psum | solution.py:256
  618.8 2.2 fusion.53
  622.0 40.7 %all-reduce.6 = (f32[768]{0:T(1024)}, f32[768]{0:T(1024)}, f32[768]{0:T(1024)}, f32[768]{0:T(1024)}, f32[768]{0:T(1024)}, /*index=5*/f32[768]{0:T(1024)}) all-reduce(f32[768]{0:T(1024)S(1)} %broadcast_multiply_fusion.7, f32[768]{0:T(1024)S(1)} %broadcast_multiply_fusion.6, ...), channel_id=1, replica_groups=mesh['dp'=8,'mp'=4] {'dp','mp'}, use_global_device_ids=true, to_apply=%region_18.19 | all-reduce | flops 4608 | bytes 36864 | tf_op jit(solution)/shard_map/psum | solution.py:244
  662.7 3.9 add_add_fusion.2
  666.6 160.3 %all-reduce.11.cloned.1.call-done = (f32[768,3,192]{0,2,1:T(8,128)}, f32[192,768]{1,0:T(8,128)}, f32[768,768]{1,0:T(8,128)}, f32[768,768]{1,0:T(8,128)}) async-done(((f32[768,3,192]{0,2,1:T(8,128)}, f32[192,768]{1,0:T(8,128)}, f32[768,768]{1,0:T(8,128)}, f32[768,768]{1,0:T(8,128)}), (f32[768,3,192]{0,2,1:T(8,128)}, f32[192,768]{1,0:T(8,128)}, f32[768,768]{1,0:T(8,128)}, ...) | async-done | bytes 7077904 | tf_op jit(solution)/shard_map/psum | solution.py:256
  826.9 2.9 copy.90
  (175 shorter events, 21.4 us)
Async XLA Ops:
  7.2 240.3 %copy-start = (bf16[768,768]{1,0:T(8,128)(2,1)S(1)}, bf16[768,768]{1,0:T(8,128)(2,1)}, u32[]{:S(2)}) copy-start(bf16[768,768]{1,0:T(8,128)(2,1)} %param.33) | copy-start | bytes 3538948
  7.2 7.6 copy-start.36
  7.2 7.7 copy-start.49
  7.2 8.1 copy-start.44
  7.2 8.1 copy-start.50
  7.2 41.0 %all-gather.5.cloned.1.call-start = ((), (), s32[]{:S(2)}) async-start(), calls=%async_computation.4 | async-start | bytes 4546560 | tf_op jit(solution)/shard_map/all_gather | solution.py:90
  8.7 2.2 copy-start.31
  14.1 164.8 %reduce-scatter.5.cloned.1.call-start = ((), (), s32[]{:S(2)}) async-start(), calls=%async_computation.5 | async-start | bytes 9093120 | tf_op jit(solution)/shard_map/reduce_scatter | solution.py:135
  15.4 44.2 %copy-start.27 = (f32[2368]{0:T(1024)}, f32[2368]{0:T(1024)S(1)}, u32[]{:S(2)}) copy-start(f32[2368]{0:T(1024)S(1)} %get-tuple-element.54) | copy-start | bytes 28420
  15.4 44.1 %copy-start.29 = (f32[2368]{0:T(1024)}, f32[2368]{0:T(1024)S(1)}, u32[]{:S(2)}) copy-start(f32[2368]{0:T(1024)S(1)} %get-tuple-element.55) | copy-start | bytes 28420
  15.4 44.1 %copy-start.40 = (f32[3,32]{1,0:T(4,128)}, f32[3,32]{1,0:T(4,128)S(1)}, u32[]{:S(2)}) copy-start(f32[3,32]{1,0:T(4,128)S(1)} %get-tuple-element.102) | copy-start | bytes 1156
  15.4 44.1 %copy-start.42 = (f32[3,32]{1,0:T(4,128)}, f32[3,32]{1,0:T(4,128)S(1)}, u32[]{:S(2)}) copy-start(f32[3,32]{1,0:T(4,128)S(1)} %get-tuple-element.103) | copy-start | bytes 1156
  16.8 81.2 %copy-start.3 = (pred[4,592,592]{1,2,0:T(8,128)(4,1)}, pred[4,592,592]{1,2,0:T(8,128)(4,1)S(1)}, u32[]{:S(2)}) copy-start(pred[4,592,592]{1,2,0:T(8,128)(4,1)S(1)} %compare_and_fusion) | copy-start | bytes 4205572
  86.8 6.2 copy-start.1
  93.0 5.0 copy-start.24
  108.0 1.5 copy-start.26
  109.5 4.1 copy-start.10
  113.7 65.2 %copy-start.46 = (f32[768]{0:T(1024)S(1)}, f32[768]{0:T(1024)}, u32[]{:S(2)}) copy-start(f32[768]{0:T(1024)} %param.28) | copy-start | bytes 9220
  113.7 67.6 %copy-start.37 = (f32[768]{0:T(1024)S(1)}, f32[768]{0:T(1024)}, u32[]{:S(2)}) copy-start(f32[768]{0:T(1024)} %param.29) | copy-start | bytes 9220
  113.7 67.6 %copy-start.47 = (f32[768]{0:T(1024)S(1)}, f32[768]{0:T(1024)}, u32[]{:S(2)}) copy-start(f32[768]{0:T(1024)} %param.30) | copy-start | bytes 9220
  113.7 100.4 %all-gather.7.cloned.1.call-start = ((), (), s32[]{:S(2)}) async-start(), calls=%async_computation.6 | async-start | bytes 4546560 | tf_op jit(solution)/shard_map/all_gather | solution.py:149
  181.3 5.3 copy-start.51
  182.6 64.9 %all-gather.9.cloned.1.call-start = ((), (), s32[]{:S(2)}) async-start(), calls=%async_computation.8 | async-start | bytes 4546560 | tf_op jit(solution)/shard_map/all_gather | solution.py:164
  186.6 155.7 %reduce-scatter.9.cloned.1.call-start = ((), (), s32[]{:S(2)}) async-start(), calls=%async_computation.9 | async-start | bytes 9093120 | tf_op jit(solution)/shard_map/reduce_scatter | solution.py:172
  247.5 24.5 %copy-start.54 = (bf16[768,768]{1,0:T(8,128)(2,1)S(1)}, bf16[768,768]{1,0:T(8,128)(2,1)}, u32[]{:S(2)}) copy-start(bf16[768,768]{1,0:T(8,128)(2,1)} %param.31) | copy-start | bytes 3538948
  270.1 1.9 copy-start.56
  277.2 108.7 %reduce-scatter.7.cloned.1.call-start = ((), (), s32[]{:S(2)}) async-start(), calls=%async_computation.7 | async-start | bytes 4546560 | tf_op jit(solution)/shard_map/reduce_scatter | solution.py:156
  283.4 1.8 copy-start.19
  289.6 96.2 %copy-start.48 = (f32[768]{0:T(1024)S(1)}, f32[768]{0:T(1024)}, u32[]{:S(2)}) copy-start(f32[768]{0:T(1024)} %param.34) | copy-start | bytes 9220
  289.6 133.8 %all-gather.11.cloned.1.call-start = ((), (), s32[]{:S(2)}) async-start(), calls=%async_computation.10 | async-start | bytes 4546560 | tf_op jit(solution)/shard_map/all_gather | solution.py:183
  385.8 4.8 copy-start.8
  389.4 1.2 copy-start.7
  391.9 226.9 %reduce-scatter.11.cloned.1.call-start = ((), (), s32[]{:S(2)}) async-start(), calls=%async_computation.11 | async-start | bytes 9093120 | tf_op jit(solution)/shard_map/reduce_scatter | solution.py:233
  392.0 39.3 %copy-start.4 = (pred[4,592,592]{1,2,0:T(8,128)(4,1)S(1)}, pred[4,592,592]{1,2,0:T(8,128)(4,1)}, u32[]{:S(2)}) copy-start(pred[4,592,592]{1,2,0:T(8,128)(4,1)} %copy-done.3) | copy-start | bytes 4205572
  462.7 13.5 %copy-start.12 = (bf16[4,592,3,64]{1,3,2,0:T(8,128)(2,1)S(1)}, bf16[4,592,3,64]{1,3,2,0:T(8,128)(2,1)}, u32[]{:S(2)}) copy-start(bf16[4,592,3,64]{1,3,2,0:T(8,128)(2,1)} %copy_dynamic-update-slice_fusion.2) | copy-start | bytes 2727940
  476.2 4.1 copy-start.13
  492.0 7.3 copy-start.5
  492.0 7.3 copy-start.28
  492.0 7.3 copy-start.30
  492.0 7.4 copy-start.41
  492.0 7.4 copy-start.43
  499.3 7.2 copy-start.6
  510.2 1.5 copy-start.14
  510.2 2.1 copy-start.55
  510.4 1.0 copy-start.15
  510.5 1.2 copy-start.17
  518.4 308.5 %all-reduce.11.cloned.1.call-start = ((), (), s32[]{:S(2)}) async-start(), calls=%async_computation.12 | async-start | bytes 14155776 | tf_op jit(solution)/shard_map/psum | solution.py:256
  559.2 8.0 copy-start.20
  559.2 8.0 copy-start.53
  567.1 4.8 copy-start.11
  567.1 4.8 copy-start.21
  567.2 6.6 copy-start.52
  572.0 1.8 copy-start.16
  572.0 1.8 copy-start.18
  577.4 0.7 copy-start.45
  577.4 41.4 %copy-start.2 = (bf16[592,768]{1,0:T(8,128)(2,1)S(1)}, bf16[592,768]{1,0:T(8,128)(2,1)}, u32[]{:S(2)}) copy-start(bf16[592,768]{1,0:T(8,128)(2,1)} %param.18) | copy-start | bytes 2727940
  577.4 41.4 %copy-start.32 = (f32[592]{0:T(1024)S(1)}, f32[592]{0:T(1024)}, u32[]{:S(2)}) copy-start(f32[592]{0:T(1024)} %copy-done.31) | copy-start | bytes 7108
  577.4 41.4 %copy-start.33 = (f32[768]{0:T(1024)S(1)}, f32[768]{0:T(1024)}, u32[]{:S(2)}) copy-start(f32[768]{0:T(1024)} %param.22) | copy-start | bytes 9220
  577.5 43.6 %copy-start.39 = (f32[592]{0:T(1024)S(1)}, f32[592]{0:T(1024)}, u32[]{:S(2)}) copy-start(f32[592]{0:T(1024)} %copy-done.38) | copy-start | bytes 7108
  577.5 43.6 %copy-start.35 = (f32[592]{0:T(1024)S(1)}, f32[592]{0:T(1024)}, u32[]{:S(2)}) copy-start(f32[592]{0:T(1024)} %copy-done.34) | copy-start | bytes 7108
  618.8 2.2 copy-start.9
  826.9 3.0 copy-start.25
  826.9 3.8 copy-start.23
  829.9 2.2 copy-start.22
  (2 other events, 1.2 us)
Sparse Core Ops, SparseCore 0:
  14.2 34.0 all-gather.4
  113.8 65.0 reduce-scatter.4
  182.7 31.3 all-gather.6
  216.1 31.3 all-gather.8
  277.3 64.9 reduce-scatter.8
  344.8 41.0 reduce-scatter.6
  392.1 31.3 all-gather.10
  518.5 65.7 reduce-scatter.10
  589.8 237.0 all-reduce.10
where the time goes:
time: 850 us; the launch traced here: 840 us
  waiting for transfers between devices  435 us (51%)
  matrix products  130 us (15%)
  blocking collectives  119 us (14%)
  other arithmetic  73.7 us (9%)
  local copies, waits for them, and re-layouts  66.3 us (8%)
  between operations  16.1 us (2%)
    psum x1, waiting for transfers between devices, body(): lax.psum((grad_w_qkv * factor, grad_b_qkv * factor, grad_freqs * factor,...  160 us
    reduce_scatter x1, waiting for transfers between devices, body(): lax.psum_scatter(jnp.dot(attended_b, w_out, preferred_element_type=jnp.fl...  65.1 us
    reduce_scatter x1, waiting for transfers between devices, body(): lax.psum_scatter(jnp.einsum('tf,df->td', grad_hidden_b, w_up, preferred_e...  52.7 us
    reduce_scatter x1, waiting for transfers between devices, body(): lax.psum_scatter(jnp.dot(active_b, w_down, preferred_element_type=jnp.flo...  41.3 us
    psum x1, blocking collectives, body(): lax.psum((grad_gain1 * factor, grad_bias1 * factor, grad_b_out * factor,...  40.7 us
    psum x1, blocking collectives, body(): counted = lax.psum(count_own, ('dp', 'mp'))  40 us
    psum x1, blocking collectives, body(): lax.psum((grad_w_qkv * factor, grad_b_qkv * factor, grad_freqs * factor,...  38.1 us
    all_gather x1, waiting for transfers between devices, body(): normed_all = lax.all_gather(normed_low, 'mp', axis=0, tiled=True)  31.5 us
  transfers between devices with their start and end apart: 9, of which 8 were waited for; matrix products, arithmetic and copies ran while one was open for 7% of the time, Pallas kernels for 0%

commit v1 on v0

v1 whole, which is shorter than its diff:
```python
import math

import jax
import jax.numpy as jnp
from jax import lax
from jax.sharding import PartitionSpec as P

HD = 64
SIDE_SMALL = 14
SIDE_LARGE = 24
IMG_SMALL = 3
IMG_LARGE = 1
NORM_EPS = 1e-06
MASK_FILL = -1e30
BF = jnp.bfloat16
F32 = jnp.float32
SCALE = 1.0 / math.sqrt(HD)


def swap(value, axis, bit):
    size = lax.axis_size(axis)
    return lax.ppermute(value, axis, [(i, i ^ bit) for i in range(size)])


def layer_norm(values, norm_gain, norm_bias):
    row_mean = jnp.mean(values, axis=-1, keepdims=True)
    centered = values - row_mean
    variance = jnp.mean(centered * centered, axis=-1, keepdims=True)
    scale = lax.rsqrt(variance + NORM_EPS)
    unit = centered * scale
    return unit * norm_gain + norm_bias, unit, scale


def norm_back(grad, unit, scale, gain):
    u = grad * gain
    mean_u = jnp.mean(u, axis=-1, keepdims=True)
    mean_un = jnp.mean(u * unit, axis=-1, keepdims=True)
    return scale * (u - mean_u - unit * mean_un)


def halves(value, upper):
    half = value.shape[0] // 2
    mine = lax.dynamic_slice_in_dim(value, upper * half, half, 0)
    other = lax.dynamic_slice_in_dim(value, (1 - upper) * half, half, 0)
    return mine, other


def join(mine, other, upper):
    return jnp.where(
        upper == 0, jnp.concatenate([mine, other]), jnp.concatenate([other, mine])
    )


def gather_weight(own):
    upper = lax.axis_index("dp") % 2
    mine, _ = halves(own, upper)
    got = swap(mine, "mp", 2)
    across = join(got, swap(got, "dp", 1), upper)
    return [own, swap(own, "mp", 1), across, swap(across, "mp", 1)]


def reduce_weight(parts):
    keep = [parts[0] + swap(parts[1], "mp", 1), parts[2] + swap(parts[3], "mp", 1)]
    total = keep[0] + swap(keep[1], "mp", 2)
    index = lax.axis_index("dp")
    size = lax.axis_size("dp")
    upper = index % 2
    mine, other = halves(total, upper)
    total = mine + swap(other, "dp", 1)
    groups = size // 2
    place = index // 2
    rows = total.shape[0] // groups
    pieces = [
        lax.dynamic_slice_in_dim(total, (place ^ step) * rows, rows, 0) for step in range(groups)
    ]
    total = pieces[0].astype(F32)
    for step in range(1, groups):
        total = total + swap(pieces[step], "dp", 2 * step).astype(F32)
    total = total.astype(BF)
    back = [total] + [swap(total, "dp", 2 * step) for step in range(1, groups)]
    stacked = jnp.stack(back)
    order = jnp.arange(groups) ^ place
    total = jnp.take(stacked, order, axis=0).reshape((groups * rows,) + total.shape[1:])
    return join(total, swap(total, "dp", 1), upper)


def reduce_small(vector):
    for axis in ("mp", "dp"):
        bit = 1
        while bit < lax.axis_size(axis):
            vector = vector + swap(vector, axis, bit)
            bit *= 2
    return vector


def turn(values, cosine, sine):
    a, b = values[..., :32], values[..., 32:]
    return jnp.concatenate([a * cosine - b * sine, b * cosine + a * sine], -1)


def dot(left, right):
    return jnp.dot(left, right, preferred_element_type=F32)


def dot_t(left, right):
    return lax.dot_general(left, right, (((0,), (0,)), ((), ())), preferred_element_type=F32)


def dot_r(left, right):
    return lax.dot_general(left, right, (((1,), (1,)), ((), ())), preferred_element_type=F32)


def gelu_both(v):
    cdf = 0.5 * (1.0 + lax.erf(v * (1.0 / math.sqrt(2.0))))
    pdf = jnp.exp(-0.5 * v * v) * (1.0 / math.sqrt(2.0 * math.pi))
    return v * cdf, cdf + v * pdf


def body(
    tokens,
    image_group,
    positions,
    keep_mask,
    norm1_gain,
    norm1_bias,
    w_qkv,
    b_qkv,
    rotary_freqs,
    w_out,
    b_out,
    norm2_gain,
    norm2_bias,
    w_up,
    b_up,
    w_down,
    b_down,
    cotangent,
):
    rows, width = tokens.shape
    parts = lax.axis_size("mp")
    mp_index = lax.axis_index("mp")
    heads = rotary_freqs.shape[1]
    local = heads * HD
    units = w_up.shape[1]
    is_large = image_group[0]
    grid_side = jnp.where(is_large == 1, SIDE_LARGE, SIDE_SMALL)
    image_count = jnp.where(is_large == 1, IMG_LARGE, IMG_SMALL)
    keep_all = keep_mask.astype(F32)
    keep_own = lax.dynamic_slice_in_dim(keep_all, mp_index * rows, rows)
    place = lax.dynamic_slice_in_dim(positions, mp_index * rows, rows, 1).astype(F32)
    inpack = jnp.arange(rows, dtype=jnp.int32)
    image_id = jnp.minimum(inpack // (grid_side * grid_side), image_count - 1)
    visible = (image_id[:, None] == image_id[None, :]) & (keep_own[None, :] > 0.5)

    small = jnp.concatenate(
        [b_qkv.reshape(-1), rotary_freqs.reshape(-1), b_up.astype(F32)]
    )
    smalls = [small, swap(small, "mp", 1), swap(small, "mp", 2), swap(small, "mp", 3)]
    qkv_parts = gather_weight(w_qkv.reshape(width, 3 * local))
    out_parts = gather_weight(w_out)
    up_parts = gather_weight(w_up)
    down_parts = gather_weight(w_down)

    x_own = tokens.astype(F32)
    normed_one, unit1, scale1 = layer_norm(x_own, norm1_gain, norm1_bias)
    normed_b = normed_one.astype(BF)
    saved = []
    branch = b_out
    for r in range(parts):
        bias = smalls[r][: 3 * local]
        freqs = smalls[r][3 * local : 3 * local + heads * HD].reshape(2, heads, HD // 2)
        angles = (
            place[0][:, None, None] * freqs[0][None] + place[1][:, None, None] * freqs[1][None]
        )
        cosine, sine = jnp.cos(angles), jnp.sin(angles)
        projected = (dot(normed_b, qkv_parts[r]) + bias).reshape(rows, 3, heads, HD)
        query = turn(projected[:, 0], cosine, sine)
        key = turn(projected[:, 1], cosine, sine)
        query_b, key_b, value_b = query.astype(BF), key.astype(BF), projected[:, 2].astype(BF)
        scores = jnp.einsum("qhd,khd->hqk", query_b, key_b, preferred_element_type=F32) * SCALE
        masked = jnp.where(visible[None], scores, MASK_FILL)
        row_max = jnp.max(masked, axis=-1, keepdims=True)
        terms = jnp.where(visible[None], jnp.exp(masked - row_max), 0.0)
        row_sum = jnp.sum(terms, axis=-1, keepdims=True)
        probs = terms / row_sum
        attended = jnp.einsum("hqk,khd->qhd", probs.astype(BF), value_b, preferred_element_type=F32)
        attended_b = attended.reshape(rows, local).astype(BF)
        branch = branch + dot(attended_b, out_parts[r])
        saved.append((query, key, query_b, key_b, value_b, probs, attended_b, cosine, sine))
    middle = x_own + branch
    normed_two, unit2, scale2 = layer_norm(middle, norm2_gain, norm2_bias)
    second_b = normed_two.astype(BF)
    grad_out = cotangent * keep_own[:, None]
    grad_out_b = grad_out.astype(BF)
    sum_b_down = jnp.sum(grad_out_b.astype(F32), axis=0)
    mlp = b_down
    grad_second = 0.0
    sums_b_up, raw_up, raw_down = [], [], []
    for r in range(parts):
        hidden = dot(second_b, up_parts[r]) + smalls[r][3 * local + heads * HD :]
        active, slope = gelu_both(hidden)
        active_b = active.astype(BF)
        mlp = mlp + dot(active_b, down_parts[r])
        raw_down.append(dot_t(active_b, grad_out_b).astype(BF))
        grad_hidden_b = (dot_r(grad_out_b, down_parts[r]) * slope).astype(BF)
        raw_up.append(dot_t(second_b, grad_hidden_b).astype(BF))
        sums_b_up.append(jnp.sum(grad_hidden_b.astype(F32), axis=0))
        grad_second = grad_second + dot_r(grad_hidden_b, up_parts[r])
    output = (middle + mlp).astype(BF)
    sum_w_down = reduce_weight(raw_down)
    sum_w_up = reduce_weight(raw_up)
    sum_gain2 = jnp.sum(grad_second * unit2, axis=0)
    sum_bias2 = jnp.sum(grad_second, axis=0)
    grad_middle = grad_out + norm_back(grad_second, unit2, scale2, norm2_gain)
    branch_b = grad_middle.astype(BF)
    sum_b_out = jnp.sum(branch_b.astype(F32), axis=0)
    sum_w_out = reduce_weight([dot_t(saved[r][6], branch_b).astype(BF) for r in range(parts)])
    grad_first = 0.0
    raw_qkv, sums_b_qkv, sums_freqs = [], [], []
    for r in range(parts):
        query, key, query_b, key_b, value_b, probs, attended_b, cosine, sine = saved[r]
        grad_att = dot_r(branch_b, out_parts[r]).astype(BF).reshape(rows, heads, HD)
        grad_probs = jnp.einsum("qhd,khd->hqk", grad_att, value_b, preferred_element_type=F32)
        grad_value = jnp.einsum(
            "hqk,qhd->khd", probs.astype(BF), grad_att, preferred_element_type=F32
        )
        inner = jnp.sum(probs * grad_probs, axis=-1, keepdims=True)
        grad_scores = (probs * (grad_probs - inner)).astype(BF)
        grad_query = (
            jnp.einsum("hqk,khd->qhd", grad_scores, key_b, preferred_element_type=F32) * SCALE
        )
        grad_key = (
            jnp.einsum("hqk,qhd->khd", grad_scores, query_b, preferred_element_type=F32) * SCALE
        )
        term = (
            grad_query[..., 32:] * query[..., :32]
            - grad_query[..., :32] * query[..., 32:]
            + grad_key[..., 32:] * key[..., :32]
            - grad_key[..., :32] * key[..., 32:]
        )
        sums_freqs.append(jnp.einsum("pt,thj->phj", place, term, precision=lax.Precision.HIGHEST))
        grad_qkv = jnp.concatenate(
            [
                turn(grad_query, cosine, -sine).reshape(rows, local),
                turn(grad_key, cosine, -sine).reshape(rows, local),
                grad_value.reshape(rows, local),
            ],
            axis=1,
        ).astype(BF)
        raw_qkv.append(dot_t(normed_b, grad_qkv).astype(BF))
        sums_b_qkv.append(jnp.sum(grad_qkv.astype(F32), axis=0))
        grad_first = grad_first + dot_r(grad_qkv, qkv_parts[r])
    sum_w_qkv = reduce_weight(raw_qkv)
    sum_gain1 = jnp.sum(grad_first * unit1, axis=0)
    sum_bias1 = jnp.sum(grad_first, axis=0)
    grad_tokens = grad_middle + norm_back(grad_first, unit1, scale1, norm1_gain)

    slot = [
        jnp.concatenate([sums_b_qkv[r], sums_freqs[r].reshape(-1), sums_b_up[r]])
        for r in range(parts)
    ]
    slots = jnp.take(jnp.stack(slot), jnp.arange(parts) ^ mp_index, axis=0)
    packed = jnp.concatenate(
        [
            jnp.stack([sum_gain1, sum_bias1, sum_b_out, sum_gain2, sum_bias2, sum_b_down]).reshape(-1),
            slots.reshape(-1),
            jnp.full((128,), jnp.sum(keep_own)),
        ]
    ).reshape(-1, 128)
    packed = reduce_small(packed).reshape(-1)
    factor = lax.axis_size("dp") / packed[-1]
    packed = packed * factor
    vectors = packed[: 6 * width].reshape(6, width)
    own = lax.dynamic_slice_in_dim(
        packed[6 * width : -128].reshape(parts, -1), mp_index, 1, 0
    )[0]
    return (
        output,
        grad_tokens,
        vectors[0],
        vectors[1],
        (sum_w_qkv.astype(F32) * factor).reshape(w_qkv.shape),
        own[: 3 * local].reshape(3, local),
        own[3 * local : 3 * local + heads * HD].reshape(rotary_freqs.shape),
        sum_w_out.astype(F32) * factor,
        vectors[2],
        vectors[3],
        vectors[4],
        sum_w_up.astype(F32) * factor,
        own[3 * local + heads * HD :],
        sum_w_down.astype(F32) * factor,
        vectors[5],
    )


def solution(mesh):
    placed = (
        P(("dp", "mp"), None),
        P("dp"),
        P(None, "dp"),
        P("dp"),
        P(),
        P(),
        P(None, None, "mp"),
        P(None, "mp"),
        P(None, "mp", None),
        P("mp", None),
        P(),
        P(),
        P(),
        P(None, "mp"),
        P("mp"),
        P("mp", None),
        P(),
        P(("dp", "mp"), None),
    )
    return jax.shard_map(
        body,
        mesh=mesh,
        in_specs=placed,
        out_specs=(
            P(("dp", "mp"), None),
            P(("dp", "mp"), None),
            P(),
            P(),
            P(None, None, "mp"),
            P(None, "mp"),
            P(None, "mp", None),
            P("mp", None),
            P(),
            P(),
            P(),
            P(None, "mp"),
            P("mp"),
            P("mp", None),
            P(),
        ),
        check_vma=False,
    )
```

time: 850 us -> 473 us (0.56)
  waiting for transfers between devices: 435 us -> 123 us
  blocking collectives: 119 us -> 0 us
  starting transfers between devices: 0.37 us -> 83.9 us
  matrix products: 130 us -> 160 us
  local copies, waits for them, and re-layouts: 66.3 us -> 41.8 us
  other arithmetic: 73.7 us -> 53.6 us
  between operations: 16.1 us -> 4.44 us
    psum x1 -> x0, waiting for transfers between devices: 160 us -> none  [body(): lax.psum((grad_w_qkv * factor, grad_b_qkv * factor, grad_freqs * factor,...]
    reduce_scatter x4 -> x0, waiting for transfers between devices: 159 us -> none  [the longest x1 65.1 us: body(): lax.psum_scatter(jnp.dot(attended_b, w_out, preferred_element_type=jnp.fl...]
    ppermute x0 -> x68, waiting for transfers between devices: none -> 123 us  [swap(): return lax.ppermute(value, axis, [(i, i ^ bit) for i in range(size)])]
    psum x3 -> x0, blocking collectives: 119 us -> none  [the longest x1 40.7 us: body(): lax.psum((grad_gain1 * factor, grad_bias1 * factor, grad_b_out * factor,...]
    all_gather x4 -> x0, waiting for transfers between devices: 115 us -> none  [the longest x1 31.5 us: body(): normed_all = lax.all_gather(normed_low, 'mp', axis=0, tiled=True)]
    ppermute x0 -> x68, starting transfers between devices: none -> 83.9 us  [swap(): return lax.ppermute(value, axis, [(i, i ^ bit) for i in range(size)])]
    sub x0 -> x4, matrix products: none -> 22.5 us  [body(): terms = jnp.where(visible[None], jnp.exp(masked - row_max), 0.0)]
    reduce_sum x10 -> x7, other arithmetic: 24.7 us -> 5.59 us  [the longest x1 2.11 us: body(): sum_b_out = jnp.sum(branch_b.astype(F32), axis=0)]
  transfers between devices with their start and end apart: 9 -> 68, of which waited for: 8 -> 22; matrix products, arithmetic and copies ran while one was open for 7% -> 40% of each run, Pallas kernels for 0% -> 0%
where the time goes in v1:
time: 473 us; the launch traced here: 467 us
  matrix products  160 us (34%)
  waiting for transfers between devices  123 us (26%)
  starting transfers between devices  83.9 us (18%)
  other arithmetic  53.6 us (11%)
  local copies, waits for them, and re-layouts  41.8 us (9%)
    ppermute x68, waiting for transfers between devices, swap(): return lax.ppermute(value, axis, [(i, i ^ bit) for i in range(size)])  123 us
    ppermute x68, starting transfers between devices, swap(): return lax.ppermute(value, axis, [(i, i ^ bit) for i in range(size)])  83.9 us
    dot_general x16, matrix products, dot(): return jnp.dot(left, right, preferred_element_type=F32)  37.4 us
    dot_general x16, matrix products, dot_r(): lax.dot_general(left, right, (((1,), (1,)), ((), ())), preferred_element_...  33.8 us
    dot_general x16, matrix products, dot_t(): lax.dot_general(left, right, (((0,), (0,)), ((), ())), preferred_element_...  28.5 us
    sub x4, matrix products, body(): terms = jnp.where(visible[None], jnp.exp(masked - row_max), 0.0)  22.5 us
    dot_general x4, matrix products, body(): jnp.einsum('hqk,khd->qhd', probs.astype(BF), value_b, preferred_element_t...  12.8 us
    another operation x8, other arithmetic  12.4 us
  transfers between devices with their start and end apart: 68, of which 22 were waited for; matrix products, arithmetic and copies ran while one was open for 40% of the time, Pallas kernels for 0%

profile of v1, /device:TPU:0, one launch (start us, length us, event | category | flops | bytes accessed | tf_op | source)
XLA Modules:
  0.0 466.9 jit_solution(15431252619958721565)
XLA Ops:
  3.5 2.5 collective-permute-start.5
  22.9 5.6 %fusion.250 = (f32[3,592]{1,0:T(4,128)S(1)}, f32[3,592,592]{1,2,0:T(8,128)}) fusion(pred[592,592]{0,1:T(8,128)(4,1)} %compare_and_fusion, bf16[592,3,32]{0,2,1:T(8,128)(2,1)S(1)} %get-tuple-element.116, bf16[592,3,32]{0,2,1:T(8,128)(2,1)} %get-tuple-element.117, bf16[592,3,32]{0,2,1:T(8,128)(2,1)} %get-tuple-element.83, ...), kind=kOutput, calls=%fused_computation.478 | convolution fusion | flops 140745040 | bytes 5017792 | tf_op jit(solution)/shard_map/sub | solution.py:183
  28.5 3.0 convolution_convert_fusion.27
  31.6 2.8 fusion.253
  46.7 25.4 %collective-permute-done.6 = bf16[96,768]{1,0:T(8,128)(2,1)S(1)} collective-permute-done((bf16[96,768]{1,0:T(8,128)(2,1)}, bf16[96,768]{1,0:T(8,128)(2,1)S(1)}, u32[]{:S(2)}, u32[]{:S(2)}) %collective-permute-start.6) | collective-permute-done | bytes 147488 | tf_op jit(solution)/shard_map/ppermute | solution.py:22
  81.5 2.2 convolution_add_fusion.2
  84.9 6.1 %collective-permute-done.4 = bf16[384,576]{0,1:T(8,128)(2,1)S(1)} collective-permute-done((bf16[384,576]{0,1:T(8,128)(2,1)S(1)}, bf16[384,576]{0,1:T(8,128)(2,1)S(1)}, u32[]{:S(2)}, u32[]{:S(2)}) %collective-permute-start.4) | collective-permute-done | bytes 442400 | tf_op jit(solution)/shard_map/ppermute | solution.py:22
  97.2 5.7 %fusion.249 = (f32[3,592]{1,0:T(4,128)S(1)}, f32[3,592,592]{1,2,0:T(8,128)}) fusion(pred[592,592]{0,1:T(8,128)(4,1)} %compare_and_fusion, bf16[592,3,32]{0,2,1:T(8,128)(2,1)} %get-tuple-element.118, bf16[592,3,32]{0,2,1:T(8,128)(2,1)} %get-tuple-element.119, bf16[592,3,32]{0,2,1:T(8,128)(2,1)} %get-tuple-element.87, bf16[592,3,32]{0,2,1:T(8,128)(2,1)} %get-tuple-element.86), kind=kOutput, calls=%fused_computation.477 | convolution fusion | flops 140745040 | bytes 5017792 | tf_op jit(solution)/shard_map/sub | solution.py:183
  102.9 3.0 convolution_convert_fusion.26
  106.0 2.3 fusion.223
  108.2 5.6 %fusion.251 = (f32[3,592]{1,0:T(4,128)S(1)}, f32[3,592,592]{1,2,0:T(8,128)}) fusion(pred[592,592]{0,1:T(8,128)(4,1)} %compare_and_fusion, bf16[592,3,32]{0,2,1:T(8,128)(2,1)S(1)} %get-tuple-element.114, bf16[592,3,32]{0,2,1:T(8,128)(2,1)S(1)} %get-tuple-element.115, bf16[592,3,32]{0,2,1:T(8,128)(2,1)} %get-tuple-element.79, ...), kind=kOutput, calls=%fused_computation.479 | convolution fusion | flops 140745040 | bytes 5017792 | tf_op jit(solution)/shard_map/sub | solution.py:183
  113.9 3.7 convolution_convert_fusion.25
  119.8 2.9 maximum_select_fusion
  123.2 2.9 maximum_select_fusion.1
  130.8 5.6 %fusion.248 = (f32[3,592]{1,0:T(4,128)S(1)}, f32[3,592,592]{1,2,0:T(8,128)}) fusion(pred[592,592]{0,1:T(8,128)(4,1)} %compare_and_fusion, bf16[592,3,32]{0,2,1:T(8,128)(2,1)S(1)} %get-tuple-element.120, bf16[592,3,32]{0,2,1:T(8,128)(2,1)S(1)} %get-tuple-element.121, bf16[592,3,32]{0,2,1:T(8,128)(2,1)S(1)} %get-tuple-element.91, ...), kind=kOutput, calls=%fused_computation.476 | convolution fusion | flops 140745040 | bytes 5017792 | tf_op jit(solution)/shard_map/sub | solution.py:183
  136.5 3.1 convolution_convert_fusion.24
  143.1 2.5 fusion.258
  145.7 2.9 multiply_convert_fusion.6
  148.6 3.2 convert_reduce_fusion.3
  151.8 2.2 convolution_convert_fusion.6
  155.0 3.2 convert_reduce_fusion.4
  159.1 3.4 fusion.256
  162.4 2.3 fusion.261
  167.0 2.2 convolution_convert_fusion.2
  169.2 3.4 fusion.257
  172.6 3.2 convert_reduce_fusion.2
  175.8 3.6 multiply_convert_fusion.4
  179.3 3.2 convert_reduce_fusion.1
  184.6 2.3 fusion.262
  187.0 3.1 multiply_reduce_fusion.4
  219.5 2.2 fusion.120
  224.2 2.2 fusion.112
  245.2 4.6 fusion.32
  259.4 2.6 fusion.259
  262.6 3.7 add_convert_fusion
  266.7 3.7 collective-permute-done.20
  279.3 4.1 collective-permute-done.37
  283.4 2.6 collective-permute-start.23
  291.5 2.4 collective-permute-done.38
  294.2 2.5 collective-permute-start.40
  296.7 8.8 %collective-permute-done.26 = bf16[768,576]{0,1:T(8,128)(2,1)S(1)} collective-permute-done((bf16[768,576]{0,1:T(8,128)(2,1)S(1)}, bf16[768,576]{0,1:T(8,128)(2,1)S(1)}, u32[]{:S(2)}, u32[]{:S(2)}) %collective-permute-start.26) | collective-permute-done | bytes 884768 | tf_op jit(solution)/shard_map/ppermute | solution.py:22
  309.1 2.2 collective-permute-done.41
  312.6 3.4 fusion.59
  316.1 4.0 collective-permute-done.27
  320.1 3.1 collective-permute-start.44
  324.5 2.3 fusion.60
  330.3 7.7 %collective-permute-done.29 = bf16[96,576]{0,1:T(8,128)(2,1)S(1)} collective-permute-done((bf16[96,576]{0,1:T(8,128)(2,1)S(1)}, bf16[96,576]{0,1:T(8,128)(2,1)S(1)}, u32[]{:S(2)}, u32[]{:S(2)}) %collective-permute-start.29) | collective-permute-done | bytes 110624 | tf_op jit(solution)/shard_map/ppermute | solution.py:22
  340.4 4.5 collective-permute-done.30
  345.2 2.4 collective-permute-start.32
  347.6 5.3 %collective-permute-done.48 = bf16[768,768]{1,0:T(8,128)(2,1)} collective-permute-done((bf16[768,768]{1,0:T(8,128)(2,1)}, bf16[768,768]{1,0:T(8,128)(2,1)}, u32[]{:S(2)}, u32[]{:S(2)}) %collective-permute-start.48) | collective-permute-done | bytes 1179680 | tf_op jit(solution)/shard_map/ppermute | solution.py:22
  353.5 3.3 fusion.64
  359.2 17.2 %collective-permute-done.59 = bf16[768,768]{1,0:T(8,128)(2,1)} collective-permute-done((bf16[768,768]{1,0:T(8,128)(2,1)}, bf16[768,768]{1,0:T(8,128)(2,1)}, u32[]{:S(2)}, u32[]{:S(2)}) %collective-permute-start.59) | collective-permute-done | bytes 1179680 | tf_op jit(solution)/shard_map/ppermute | solution.py:22
  385.3 2.9 collective-permute-start.52
  388.2 5.0 %collective-permute-done.60 = bf16[384,768]{1,0:T(8,128)(2,1)} collective-permute-done((bf16[384,768]{1,0:T(8,128)(2,1)}, bf16[384,768]{1,0:T(8,128)(2,1)}, u32[]{:S(2)}, u32[]{:S(2)}) %collective-permute-start.60) | collective-permute-done | bytes 589856 | tf_op jit(solution)/shard_map/ppermute | solution.py:22
  395.8 3.1 collective-permute-start.63
  399.0 10.6 %collective-permute-start.53 = (bf16[96,768]{1,0:T(8,128)(2,1)S(1)}, bf16[96,768]{1,0:T(8,128)(2,1)S(1)}, u32[]{:S(2)}, u32[]{:S(2)}) collective-permute-start(bf16[96,768]{1,0:T(8,128)(2,1)S(1)} %add_convert_fusion.3), channel_id=1, source_target_pairs={{0,8},{4,12},{8,0},{12,4},{16,24},{20,28},{24,16},{28,20},{1,9},{5... | collective-permute-start | bytes 442376 | tf_op jit(solution)/shard_map/ppermute | solution.py:22
  409.6 2.4 collective-permute-start.55
  412.9 10.0 %collective-permute-start.64 = (bf16[96,768]{1,0:T(8,128)(2,1)S(1)}, bf16[96,768]{1,0:T(8,128)(2,1)S(1)}, u32[]{:S(2)}, u32[]{:S(2)}) collective-permute-start(bf16[96,768]{1,0:T(8,128)(2,1)S(1)} %add_convert_fusion.2), channel_id=1, source_target_pairs={{0,8},{4,12},{8,0},{12,4},{16,24},{20,28},{24,16},{28,20},{1,9},{5... | collective-permute-start | bytes 442376 | tf_op jit(solution)/shard_map/ppermute | solution.py:22
  423.0 2.4 collective-permute-start.66
  426.3 3.0 collective-permute-start.45
  430.2 4.3 collective-permute-done.65
  445.1 9.6 %collective-permute-done.67 = bf16[384,768]{1,0:T(8,128)(2,1)S(1)} collective-permute-done((bf16[384,768]{1,0:T(8,128)(2,1)S(1)}, bf16[384,768]{1,0:T(8,128)(2,1)S(1)}, u32[]{:S(2)}, u32[]{:S(2)}) %collective-permute-start.67) | collective-permute-done | bytes 589856 | tf_op jit(solution)/shard_map/ppermute | solution.py:22
  456.4 7.4 %collective-permute-done.56 = bf16[384,768]{1,0:T(8,128)(2,1)} collective-permute-done((bf16[384,768]{1,0:T(8,128)(2,1)S(1)}, bf16[384,768]{1,0:T(8,128)(2,1)}, u32[]{:S(2)}, u32[]{:S(2)}) %collective-permute-start.56) | collective-permute-done | bytes 589856 | tf_op jit(solution)/shard_map/ppermute | solution.py:22
  463.8 2.9 convert_multiply_fusion.1
  (613 shorter events, 181.1 us)
Async XLA Ops:
  3.0 41.0 %collective-permute-start.1 = (f32[1536]{0:T(1024)S(1)}, f32[1536]{0:T(1024)S(1)}, u32[]{:S(2)}, u32[]{:S(2)}) collective-permute-start(f32[1536]{0:T(1024)S(1)} %concatenate.152), channel_id=1, source_target_pairs={{0,1},{1,0},{2,3},{3,2},{4,5},{5,4},{6,7},{7,6},{8,9},{9,8},{10,11... | collective-permute-start | bytes 18440 | tf_op jit(solution)/shard_map/ppermute | solution.py:22
  3.5 40.8 %collective-permute-start.5 = (f32[1536]{0:T(1024)S(1)}, f32[1536]{0:T(1024)S(1)}, u32[]{:S(2)}, u32[]{:S(2)}) collective-permute-start(f32[1536]{0:T(1024)S(1)} %concatenate.152), channel_id=1, source_target_pairs={{0,2},{1,3},{2,0},{3,1},{4,6},{5,7},{6,4},{7,5},{8,10},{9,11},{10,... | collective-permute-start | bytes 18440 | tf_op jit(solution)/shard_map/ppermute | solution.py:22
  6.0 40.2 %collective-permute-start.9 = (f32[1536]{0:T(1024)S(1)}, f32[1536]{0:T(1024)S(1)}, u32[]{:S(2)}, u32[]{:S(2)}) collective-permute-start(f32[1536]{0:T(1024)S(1)} %concatenate.152), channel_id=1, source_target_pairs={{0,3},{1,2},{2,1},{3,0},{4,7},{5,6},{6,5},{7,4},{8,11},{9,10},{10,... | collective-permute-start | bytes 18440 | tf_op jit(solution)/shard_map/ppermute | solution.py:22
  6.1 73.8 %collective-permute-start = (bf16[768,576]{0,1:T(8,128)(2,1)}, bf16[768,576]{0,1:T(8,128)(2,1)}, u32[]{:S(2)}, u32[]{:S(2)}) collective-permute-start(bf16[768,576]{0,1:T(8,128)(2,1)} %bitcast.324), channel_id=1, source_target_pairs={{0,1},{1,0},{2,3},{3,2},{4,5},{5,4},{6,7},{7,6},{8,9},{9,8},{10,11... | collective-permute-start | bytes 2654216 | tf_op jit(solution)/shard_map/ppermute | solution.py:22
  8.2 69.8 %collective-permute-start.13 = (bf16[384,768]{1,0:T(8,128)(2,1)}, bf16[384,768]{1,0:T(8,128)(2,1)}, u32[]{:S(2)}, u32[]{:S(2)}) collective-permute-start(bf16[384,768]{1,0:T(8,128)(2,1)} %constant_dynamic-slice_fusion.18), channel_id=1, source_target_pairs={{0,2},{1,3},{2,0},{3,1},{4,6},{5,7},{6,4},{7,5},{8,10},{9,11},{10,... | collective-permute-start | bytes 1769480 | tf_op jit(solution)/shard_map/ppermute | solution.py:22
  44.1 35.4 %collective-permute-start.15 = (bf16[384,768]{1,0:T(8,128)(2,1)}, bf16[384,768]{1,0:T(8,128)(2,1)}, u32[]{:S(2)}, u32[]{:S(2)}) collective-permute-start(bf16[384,768]{1,0:T(8,128)(2,1)} %constant_dynamic-slice_fusion.17), channel_id=1, source_target_pairs={{0,2},{1,3},{2,0},{3,1},{4,6},{5,7},{6,4},{7,5},{8,10},{9,11},{10,... | collective-permute-start | bytes 1769480 | tf_op jit(solution)/shard_map/ppermute | solution.py:22
  44.3 33.1 %collective-permute-start.3 = (bf16[384,576]{0,1:T(8,128)(2,1)}, bf16[384,576]{0,1:T(8,128)(2,1)S(1)}, u32[]{:S(2)}, u32[]{:S(2)}) collective-permute-start(bf16[384,576]{0,1:T(8,128)(2,1)} %constant_dynamic-slice_fusion.20), channel_id=1, source_target_pairs={{0,2},{1,3},{2,0},{3,1},{4,6},{5,7},{6,4},{7,5},{8,10},{9,11},{10,... | collective-permute-start | bytes 1327112 | tf_op jit(solution)/shard_map/ppermute | solution.py:22
  46.2 25.9 %collective-permute-start.6 = (bf16[96,768]{1,0:T(8,128)(2,1)}, bf16[96,768]{1,0:T(8,128)(2,1)S(1)}, u32[]{:S(2)}, u32[]{:S(2)}) collective-permute-start(bf16[96,768]{1,0:T(8,128)(2,1)} %constant_dynamic-slice_fusion.19), channel_id=1, source_target_pairs={{0,2},{1,3},{2,0},{3,1},{4,6},{5,7},{6,4},{7,5},{8,10},{9,11},{10,... | collective-permute-start | bytes 442376 | tf_op jit(solution)/shard_map/ppermute | solution.py:22
  72.1 5.1 %collective-permute-start.7 = (bf16[96,768]{1,0:T(8,128)(2,1)S(1)}, bf16[96,768]{1,0:T(8,128)(2,1)S(1)}, u32[]{:S(2)}, u32[]{:S(2)}) collective-permute-start(bf16[96,768]{1,0:T(8,128)(2,1)S(1)} %collective-permute-done.6), channel_id=1, source_target_pairs={{0,4},{4,0},{8,12},{12,8},{16,20},{20,16},{24,28},{28,24},{1,5},{5... | collective-permute-start | bytes 442376 | tf_op jit(solution)/shard_map/ppermute | solution.py:22
  77.3 40.3 %collective-permute-start.2 = (bf16[192,768]{1,0:T(8,128)(2,1)}, bf16[192,768]{1,0:T(8,128)(2,1)S(1)}, u32[]{:S(2)}, u32[]{:S(2)}) collective-permute-start(bf16[192,768]{1,0:T(8,128)(2,1)} %param.29), channel_id=1, source_target_pairs={{0,1},{1,0},{2,3},{3,2},{4,5},{5,4},{6,7},{7,6},{8,9},{9,8},{10,11... | collective-permute-start | bytes 884744 | tf_op jit(solution)/shard_map/ppermute | solution.py:22
  77.4 68.2 %collective-permute-start.11 = (bf16[768,768]{1,0:T(8,128)(2,1)}, bf16[768,768]{1,0:T(8,128)(2,1)}, u32[]{:S(2)}, u32[]{:S(2)}) collective-permute-start(bf16[768,768]{1,0:T(8,128)(2,1)} %param.33), channel_id=1, source_target_pairs={{0,1},{1,0},{2,3},{3,2},{4,5},{5,4},{6,7},{7,6},{8,9},{9,8},{10,11... | collective-permute-start | bytes 3538952 | tf_op jit(solution)/shard_map/ppermute | solution.py:22
  78.0 13.0 %collective-permute-start.4 = (bf16[384,576]{0,1:T(8,128)(2,1)S(1)}, bf16[384,576]{0,1:T(8,128)(2,1)S(1)}, u32[]{:S(2)}, u32[]{:S(2)}) collective-permute-start(bf16[384,576]{0,1:T(8,128)(2,1)S(1)} %collective-permute-done.3), channel_id=1, source_target_pairs={{0,4},{4,0},{8,12},{12,8},{16,20},{20,16},{24,28},{28,24},{1,5},{5... | collective-permute-start | bytes 1327112 | tf_op jit(solution)/shard_map/ppermute | solution.py:22
  79.5 40.4 %collective-permute-start.14 = (bf16[384,768]{1,0:T(8,128)(2,1)}, bf16[384,768]{1,0:T(8,128)(2,1)}, u32[]{:S(2)}, u32[]{:S(2)}) collective-permute-start(bf16[384,768]{1,0:T(8,128)(2,1)} %collective-permute-done.13), channel_id=1, source_target_pairs={{0,4},{4,0},{8,12},{12,8},{16,20},{20,16},{24,28},{28,24},{1,5},{5... | collective-permute-start | bytes 1769480 | tf_op jit(solution)/shard_map/ppermute | solution.py:22
  80.0 42.7 %collective-permute-start.16 = (bf16[384,768]{1,0:T(8,128)(2,1)}, bf16[384,768]{1,0:T(8,128)(2,1)}, u32[]{:S(2)}, u32[]{:S(2)}) collective-permute-start(bf16[384,768]{1,0:T(8,128)(2,1)} %collective-permute-done.15), channel_id=1, source_target_pairs={{0,4},{4,0},{8,12},{12,8},{16,20},{20,16},{24,28},{28,24},{1,5},{5... | collective-permute-start | bytes 1769480 | tf_op jit(solution)/shard_map/ppermute | solution.py:22
  92.1 34.0 %collective-permute-start.8 = (bf16[768,576]{0,1:T(8,128)(2,1)}, bf16[768,576]{0,1:T(8,128)(2,1)}, u32[]{:S(2)}, u32[]{:S(2)}) collective-permute-start(bf16[768,576]{0,1:T(8,128)(2,1)} %maximum_select_fusion.4), channel_id=1, source_target_pairs={{0,1},{1,0},{2,3},{3,2},{4,5},{5,4},{6,7},{7,6},{8,9},{9,8},{10,11... | collective-permute-start | bytes 2654216 | tf_op jit(solution)/shard_map/ppermute | solution.py:22
  117.6 31.0 %collective-permute-start.12 = (bf16[768,768]{1,0:T(8,128)(2,1)}, bf16[768,768]{1,0:T(8,128)(2,1)}, u32[]{:S(2)}, u32[]{:S(2)}) collective-permute-start(bf16[768,768]{1,0:T(8,128)(2,1)} %param.35), channel_id=1, source_target_pairs={{0,1},{1,0},{2,3},{3,2},{4,5},{5,4},{6,7},{7,6},{8,9},{9,8},{10,11... | collective-permute-start | bytes 3538952 | tf_op jit(solution)/shard_map/ppermute | solution.py:22
  119.8 19.8 %collective-permute-start.10 = (bf16[192,768]{1,0:T(8,128)(2,1)S(1)}, bf16[192,768]{1,0:T(8,128)(2,1)S(1)}, u32[]{:S(2)}, u32[]{:S(2)}) collective-permute-start(bf16[192,768]{1,0:T(8,128)(2,1)S(1)} %maximum_select_fusion.6), channel_id=1, source_target_pairs={{0,1},{1,0},{2,3},{3,2},{4,5},{5,4},{6,7},{7,6},{8,9},{9,8},{10,11... | collective-permute-start | bytes 884744 | tf_op jit(solution)/shard_map/ppermute | solution.py:22
  122.7 53.0 %collective-permute-start.17 = (bf16[768,768]{1,0:T(8,128)(2,1)}, bf16[768,768]{1,0:T(8,128)(2,1)}, u32[]{:S(2)}, u32[]{:S(2)}) collective-permute-start(bf16[768,768]{1,0:T(8,128)(2,1)} %maximum_select_fusion), channel_id=1, source_target_pairs={{0,1},{1,0},{2,3},{3,2},{4,5},{5,4},{6,7},{7,6},{8,9},{9,8},{10,11... | collective-permute-start | bytes 3538952 | tf_op jit(solution)/shard_map/ppermute | solution.py:22
  126.2 53.1 %collective-permute-start.18 = (bf16[768,768]{1,0:T(8,128)(2,1)}, bf16[768,768]{1,0:T(8,128)(2,1)}, u32[]{:S(2)}, u32[]{:S(2)}) collective-permute-start(bf16[768,768]{1,0:T(8,128)(2,1)} %maximum_select_fusion.1), channel_id=1, source_target_pairs={{0,1},{1,0},{2,3},{3,2},{4,5},{5,4},{6,7},{7,6},{8,9},{9,8},{10,11... | collective-permute-start | bytes 3538952 | tf_op jit(solution)/shard_map/ppermute | solution.py:22
  240.3 71.1 %collective-permute-start.47 = (bf16[768,768]{1,0:T(8,128)(2,1)}, bf16[768,768]{1,0:T(8,128)(2,1)}, u32[]{:S(2)}, u32[]{:S(2)}) collective-permute-start(bf16[768,768]{1,0:T(8,128)(2,1)} %convolution_convert_fusion.4), channel_id=1, source_target_pairs={{0,1},{1,0},{2,3},{3,2},{4,5},{5,4},{6,7},{7,6},{8,9},{9,8},{10,11... | collective-permute-start | bytes 3538952 | tf_op jit(solution)/shard_map/ppermute | solution.py:22
  258.3 8.0 %collective-permute-start.19 = (f32[85,128]{1,0:T(8,128)S(1)}, f32[85,128]{1,0:T(8,128)S(1)}, u32[]{:S(2)}, u32[]{:S(2)}) collective-permute-start(f32[85,128]{1,0:T(8,128)S(1)} %maximum_bitcast_fusion), channel_id=1, source_target_pairs={{0,1},{1,0},{2,3},{3,2},{4,5},{5,4},{6,7},{7,6},{8,9},{9,8},{10,11... | collective-permute-start | bytes 130568 | tf_op jit(solution)/shard_map/ppermute | solution.py:22
  258.4 17.8 %collective-permute-start.36 = (bf16[192,768]{1,0:T(8,128)(2,1)}, bf16[192,768]{1,0:T(8,128)(2,1)S(1)}, u32[]{:S(2)}, u32[]{:S(2)}) collective-permute-start(bf16[192,768]{1,0:T(8,128)(2,1)} %convolution_convert_fusion.12), channel_id=1, source_target_pairs={{0,1},{1,0},{2,3},{3,2},{4,5},{5,4},{6,7},{7,6},{8,9},{9,8},{10,11... | collective-permute-start | bytes 884744 | tf_op jit(solution)/shard_map/ppermute | solution.py:22
  258.9 19.9 %collective-permute-start.35 = (bf16[192,768]{1,0:T(8,128)(2,1)}, bf16[192,768]{1,0:T(8,128)(2,1)S(1)}, u32[]{:S(2)}, u32[]{:S(2)}) collective-permute-start(bf16[192,768]{1,0:T(8,128)(2,1)} %convolution_convert_fusion.14), channel_id=1, source_target_pairs={{0,1},{1,0},{2,3},{3,2},{4,5},{5,4},{6,7},{7,6},{8,9},{9,8},{10,11... | collective-permute-start | bytes 884744 | tf_op jit(solution)/shard_map/ppermute | solution.py:22
  258.9 27.5 %collective-permute-start.25 = (bf16[768,576]{0,1:T(8,128)(2,1)}, bf16[768,576]{0,1:T(8,128)(2,1)S(1)}, u32[]{:S(2)}, u32[]{:S(2)}) collective-permute-start(bf16[768,576]{0,1:T(8,128)(2,1)} %convolution_convert_fusion.8), channel_id=1, source_target_pairs={{0,1},{1,0},{2,3},{3,2},{4,5},{5,4},{6,7},{7,6},{8,9},{9,8},{10,11... | collective-permute-start | bytes 2654216 | tf_op jit(solution)/shard_map/ppermute | solution.py:22
  276.6 6.8 %collective-permute-start.37 = (bf16[192,768]{1,0:T(8,128)(2,1)S(1)}, bf16[192,768]{1,0:T(8,128)(2,1)S(1)}, u32[]{:S(2)}, u32[]{:S(2)}) collective-permute-start(bf16[192,768]{1,0:T(8,128)(2,1)S(1)} %fusion.75), channel_id=1, source_target_pairs={{0,2},{1,3},{2,0},{3,1},{4,6},{5,7},{6,4},{7,5},{8,10},{9,11},{10,... | collective-permute-start | bytes 884744 | tf_op jit(solution)/shard_map/ppermute | solution.py:22
  278.7 45.8 %collective-permute-start.58 = (bf16[768,768]{1,0:T(8,128)(2,1)S(1)}, bf16[768,768]{1,0:T(8,128)(2,1)S(1)}, u32[]{:S(2)}, u32[]{:S(2)}) collective-permute-start(bf16[768,768]{1,0:T(8,128)(2,1)S(1)} %convolution_convert_fusion), channel_id=1, source_target_pairs={{0,1},{1,0},{2,3},{3,2},{4,5},{5,4},{6,7},{7,6},{8,9},{9,8},{10,11... | collective-permute-start | bytes 3538952 | tf_op jit(solution)/shard_map/ppermute | solution.py:22
  278.8 15.4 %collective-permute-start.24 = (bf16[768,576]{0,1:T(8,128)(2,1)S(1)}, bf16[768,576]{0,1:T(8,128)(2,1)S(1)}, u32[]{:S(2)}, u32[]{:S(2)}) collective-permute-start(bf16[768,576]{0,1:T(8,128)(2,1)S(1)} %copy-done.128), channel_id=1, source_target_pairs={{0,1},{1,0},{2,3},{3,2},{4,5},{5,4},{6,7},{7,6},{8,9},{9,8},{10,11... | collective-permute-start | bytes 2654216 | tf_op jit(solution)/shard_map/ppermute | solution.py:22
  283.4 5.3 %collective-permute-start.23 = (f32[85,128]{1,0:T(8,128)S(1)}, f32[85,128]{1,0:T(8,128)S(1)}, u32[]{:S(2)}, u32[]{:S(2)}) collective-permute-start(f32[85,128]{1,0:T(8,128)S(1)} %add.558), channel_id=1, source_target_pairs={{0,16},{4,20},{8,24},{12,28},{16,0},{20,4},{24,8},{28,12},{1,17},{... | collective-permute-start | bytes 130568 | tf_op jit(solution)/shard_map/ppermute | solution.py:22
  287.6 17.9 %collective-permute-start.26 = (bf16[768,576]{0,1:T(8,128)(2,1)S(1)}, bf16[768,576]{0,1:T(8,128)(2,1)S(1)}, u32[]{:S(2)}, u32[]{:S(2)}) collective-permute-start(bf16[768,576]{0,1:T(8,128)(2,1)S(1)} %fusion.62), channel_id=1, source_target_pairs={{0,2},{1,3},{2,0},{3,1},{4,6},{5,7},{6,4},{7,5},{8,10},{9,11},{10,... | collective-permute-start | bytes 2654216 | tf_op jit(solution)/shard_map/ppermute | solution.py:22
  294.0 13.4 %collective-permute-start.39 = (bf16[24,768]{1,0:T(8,128)(2,1)S(1)}, bf16[24,768]{1,0:T(8,128)(2,1)S(1)}, u32[]{:S(2)}, u32[]{:S(2)}) collective-permute-start(bf16[24,768]{1,0:T(8,128)(2,1)S(1)} %get-tuple-element.97), channel_id=1, source_target_pairs={{0,8},{4,12},{8,0},{12,4},{16,24},{20,28},{24,16},{28,20},{1,9},{5... | collective-permute-start | bytes 110600 | tf_op jit(solution)/shard_map/ppermute | solution.py:22
  294.2 13.3 %collective-permute-start.40 = (bf16[24,768]{1,0:T(8,128)(2,1)S(1)}, bf16[24,768]{1,0:T(8,128)(2,1)S(1)}, u32[]{:S(2)}, u32[]{:S(2)}) collective-permute-start(bf16[24,768]{1,0:T(8,128)(2,1)S(1)} %get-tuple-element.99), channel_id=1, source_target_pairs={{0,16},{4,20},{8,24},{12,28},{16,0},{20,4},{24,8},{28,12},{1,17},{... | collective-permute-start | bytes 110600 | tf_op jit(solution)/shard_map/ppermute | solution.py:22
  305.5 5.8 %collective-permute-start.41 = (bf16[24,768]{1,0:T(8,128)(2,1)S(1)}, bf16[24,768]{1,0:T(8,128)(2,1)S(1)}, u32[]{:S(2)}, u32[]{:S(2)}) collective-permute-start(bf16[24,768]{1,0:T(8,128)(2,1)S(1)} %get-tuple-element.98), channel_id=1, source_target_pairs={{0,24},{4,28},{8,16},{12,20},{16,8},{20,12},{24,0},{28,4},{1,25},{... | collective-permute-start | bytes 110600 | tf_op jit(solution)/shard_map/ppermute | solution.py:22
  307.4 37.7 %collective-permute-start.46 = (bf16[768,768]{1,0:T(8,128)(2,1)}, bf16[768,768]{1,0:T(8,128)(2,1)}, u32[]{:S(2)}, u32[]{:S(2)}) collective-permute-start(bf16[768,768]{1,0:T(8,128)(2,1)} %convolution_convert_fusion.6), channel_id=1, source_target_pairs={{0,1},{1,0},{2,3},{3,2},{4,5},{5,4},{6,7},{7,6},{8,9},{9,8},{10,11... | collective-permute-start | bytes 3538952 | tf_op jit(solution)/shard_map/ppermute | solution.py:22
  307.5 12.6 %collective-permute-start.27 = (bf16[384,576]{0,1:T(8,128)(2,1)S(1)}, bf16[384,576]{0,1:T(8,128)(2,1)S(1)}, u32[]{:S(2)}, u32[]{:S(2)}) collective-permute-start(bf16[384,576]{0,1:T(8,128)(2,1)S(1)} %constant_dynamic-slice_fusion.16), channel_id=1, source_target_pairs={{0,4},{4,0},{8,12},{12,8},{16,20},{20,16},{24,28},{28,24},{1,5},{5... | collective-permute-start | bytes 1327112 | tf_op jit(solution)/shard_map/ppermute | solution.py:22
  311.3 12.2 %collective-permute-start.42 = (bf16[24,768]{1,0:T(8,128)(2,1)S(1)}, bf16[24,768]{1,0:T(8,128)(2,1)S(1)}, u32[]{:S(2)}, u32[]{:S(2)}) collective-permute-start(bf16[24,768]{1,0:T(8,128)(2,1)S(1)} %add_convert_fusion.13), channel_id=1, source_target_pairs={{0,8},{4,12},{8,0},{12,4},{16,24},{20,28},{24,16},{28,20},{1,9},{5... | collective-permute-start | bytes 110600 | tf_op jit(solution)/shard_map/ppermute | solution.py:22
  311.4 15.4 %collective-permute-start.43 = (bf16[24,768]{1,0:T(8,128)(2,1)S(1)}, bf16[24,768]{1,0:T(8,128)(2,1)S(1)}, u32[]{:S(2)}, u32[]{:S(2)}) collective-permute-start(bf16[24,768]{1,0:T(8,128)(2,1)S(1)} %add_convert_fusion.13), channel_id=1, source_target_pairs={{0,16},{4,20},{8,24},{12,28},{16,0},{20,4},{24,8},{28,12},{1,17},{... | collective-permute-start | bytes 110600 | tf_op jit(solution)/shard_map/ppermute | solution.py:22
  320.1 6.7 %collective-permute-start.44 = (bf16[24,768]{1,0:T(8,128)(2,1)S(1)}, bf16[24,768]{1,0:T(8,128)(2,1)S(1)}, u32[]{:S(2)}, u32[]{:S(2)}) collective-permute-start(bf16[24,768]{1,0:T(8,128)(2,1)S(1)} %add_convert_fusion.13), channel_id=1, source_target_pairs={{0,24},{4,28},{8,16},{12,20},{16,8},{20,12},{24,0},{28,4},{1,25},{... | collective-permute-start | bytes 110600 | tf_op jit(solution)/shard_map/ppermute | solution.py:22
  323.6 29.3 %collective-permute-start.48 = (bf16[768,768]{1,0:T(8,128)(2,1)}, bf16[768,768]{1,0:T(8,128)(2,1)}, u32[]{:S(2)}, u32[]{:S(2)}) collective-permute-start(bf16[768,768]{1,0:T(8,128)(2,1)} %fusion.59), channel_id=1, source_target_pairs={{0,2},{1,3},{2,0},{3,1},{4,6},{5,7},{6,4},{7,5},{8,10},{9,11},{10,... | collective-permute-start | bytes 3538952 | tf_op jit(solution)/shard_map/ppermute | solution.py:22
  324.5 5.1 %collective-permute-start.28 = (bf16[96,576]{0,1:T(8,128)(2,1)S(1)}, bf16[96,576]{0,1:T(8,128)(2,1)S(1)}, u32[]{:S(2)}, u32[]{:S(2)}) collective-permute-start(bf16[96,576]{0,1:T(8,128)(2,1)S(1)} %get-tuple-element.94), channel_id=1, source_target_pairs={{0,8},{4,12},{8,0},{12,4},{16,24},{20,28},{24,16},{28,20},{1,9},{5... | collective-permute-start | bytes 331784 | tf_op jit(solution)/shard_map/ppermute | solution.py:22
  326.8 30.9 %collective-permute-start.57 = (bf16[768,768]{1,0:T(8,128)(2,1)}, bf16[768,768]{1,0:T(8,128)(2,1)S(1)}, u32[]{:S(2)}, u32[]{:S(2)}) collective-permute-start(bf16[768,768]{1,0:T(8,128)(2,1)} %convolution_convert_fusion.2), channel_id=1, source_target_pairs={{0,1},{1,0},{2,3},{3,2},{4,5},{5,4},{6,7},{7,6},{8,9},{9,8},{10,11... | collective-permute-start | bytes 3538952 | tf_op jit(solution)/shard_map/ppermute | solution.py:22
  326.8 49.6 %collective-permute-start.59 = (bf16[768,768]{1,0:T(8,128)(2,1)}, bf16[768,768]{1,0:T(8,128)(2,1)}, u32[]{:S(2)}, u32[]{:S(2)}) collective-permute-start(bf16[768,768]{1,0:T(8,128)(2,1)} %fusion.60), channel_id=1, source_target_pairs={{0,2},{1,3},{2,0},{3,1},{4,6},{5,7},{6,4},{7,5},{8,10},{9,11},{10,... | collective-permute-start | bytes 3538952 | tf_op jit(solution)/shard_map/ppermute | solution.py:22
  329.7 8.3 %collective-permute-start.29 = (bf16[96,576]{0,1:T(8,128)(2,1)S(1)}, bf16[96,576]{0,1:T(8,128)(2,1)S(1)}, u32[]{:S(2)}, u32[]{:S(2)}) collective-permute-start(bf16[96,576]{0,1:T(8,128)(2,1)S(1)} %get-tuple-element.96), channel_id=1, source_target_pairs={{0,16},{4,20},{8,24},{12,28},{16,0},{20,4},{24,8},{28,12},{1,17},{... | collective-permute-start | bytes 331784 | tf_op jit(solution)/shard_map/ppermute | solution.py:22
  338.0 6.9 %collective-permute-start.30 = (bf16[96,576]{0,1:T(8,128)(2,1)S(1)}, bf16[96,576]{0,1:T(8,128)(2,1)S(1)}, u32[]{:S(2)}, u32[]{:S(2)}) collective-permute-start(bf16[96,576]{0,1:T(8,128)(2,1)S(1)} %get-tuple-element.95), channel_id=1, source_target_pairs={{0,24},{4,28},{8,16},{12,20},{16,8},{20,12},{24,0},{28,4},{1,25},{... | collective-permute-start | bytes 331784 | tf_op jit(solution)/shard_map/ppermute | solution.py:22
  345.1 36.1 %collective-permute-start.31 = (bf16[96,576]{0,1:T(8,128)(2,1)S(1)}, bf16[96,576]{0,1:T(8,128)(2,1)S(1)}, u32[]{:S(2)}, u32[]{:S(2)}) collective-permute-start(bf16[96,576]{0,1:T(8,128)(2,1)S(1)} %add_convert_fusion.4), channel_id=1, source_target_pairs={{0,8},{4,12},{8,0},{12,4},{16,24},{20,28},{24,16},{28,20},{1,9},{5... | collective-permute-start | bytes 331784 | tf_op jit(solution)/shard_map/ppermute | solution.py:22
  345.2 36.0 %collective-permute-start.32 = (bf16[96,576]{0,1:T(8,128)(2,1)S(1)}, bf16[96,576]{0,1:T(8,128)(2,1)S(1)}, u32[]{:S(2)}, u32[]{:S(2)}) collective-permute-start(bf16[96,576]{0,1:T(8,128)(2,1)S(1)} %add_convert_fusion.4), channel_id=1, source_target_pairs={{0,16},{4,20},{8,24},{12,28},{16,0},{20,4},{24,8},{28,12},{1,17},{... | collective-permute-start | bytes 331784 | tf_op jit(solution)/shard_map/ppermute | solution.py:22
  352.8 28.3 %collective-permute-start.33 = (bf16[96,576]{0,1:T(8,128)(2,1)S(1)}, bf16[96,576]{0,1:T(8,128)(2,1)S(1)}, u32[]{:S(2)}, u32[]{:S(2)}) collective-permute-start(bf16[96,576]{0,1:T(8,128)(2,1)S(1)} %add_convert_fusion.4), channel_id=1, source_target_pairs={{0,24},{4,28},{8,16},{12,20},{16,8},{20,12},{24,0},{28,4},{1,25},{... | collective-permute-start | bytes 331784 | tf_op jit(solution)/shard_map/ppermute | solution.py:22
  357.7 24.7 %collective-permute-start.49 = (bf16[384,768]{1,0:T(8,128)(2,1)}, bf16[384,768]{1,0:T(8,128)(2,1)}, u32[]{:S(2)}, u32[]{:S(2)}) collective-permute-start(bf16[384,768]{1,0:T(8,128)(2,1)} %constant_dynamic-slice_fusion.8), channel_id=1, source_target_pairs={{0,4},{4,0},{8,12},{12,8},{16,20},{20,16},{24,28},{28,24},{1,5},{5... | collective-permute-start | bytes 1769480 | tf_op jit(solution)/shard_map/ppermute | solution.py:22
  379.2 14.0 %collective-permute-start.60 = (bf16[384,768]{1,0:T(8,128)(2,1)}, bf16[384,768]{1,0:T(8,128)(2,1)}, u32[]{:S(2)}, u32[]{:S(2)}) collective-permute-start(bf16[384,768]{1,0:T(8,128)(2,1)} %constant_dynamic-slice_fusion.4), channel_id=1, source_target_pairs={{0,4},{4,0},{8,12},{12,8},{16,20},{20,16},{24,28},{28,24},{1,5},{5... | collective-permute-start | bytes 1769480 | tf_op jit(solution)/shard_map/ppermute | solution.py:22
  383.7 12.0 %collective-permute-start.50 = (bf16[96,768]{1,0:T(8,128)(2,1)S(1)}, bf16[96,768]{1,0:T(8,128)(2,1)S(1)}, u32[]{:S(2)}, u32[]{:S(2)}) collective-permute-start(bf16[96,768]{1,0:T(8,128)(2,1)S(1)} %get-tuple-element.59), channel_id=1, source_target_pairs={{0,8},{4,12},{8,0},{12,4},{16,24},{20,28},{24,16},{28,20},{1,9},{5... | collective-permute-start | bytes 442376 | tf_op jit(solution)/shard_map/ppermute | solution.py:22
  383.8 15.1 %collective-permute-start.51 = (bf16[96,768]{1,0:T(8,128)(2,1)S(1)}, bf16[96,768]{1,0:T(8,128)(2,1)S(1)}, u32[]{:S(2)}, u32[]{:S(2)}) collective-permute-start(bf16[96,768]{1,0:T(8,128)(2,1)S(1)} %get-tuple-element.61), channel_id=1, source_target_pairs={{0,16},{4,20},{8,24},{12,28},{16,0},{20,4},{24,8},{28,12},{1,17},{... | collective-permute-start | bytes 442376 | tf_op jit(solution)/shard_map/ppermute | solution.py:22
  385.3 13.6 %collective-permute-start.52 = (bf16[96,768]{1,0:T(8,128)(2,1)S(1)}, bf16[96,768]{1,0:T(8,128)(2,1)S(1)}, u32[]{:S(2)}, u32[]{:S(2)}) collective-permute-start(bf16[96,768]{1,0:T(8,128)(2,1)S(1)} %get-tuple-element.60), channel_id=1, source_target_pairs={{0,24},{4,28},{8,16},{12,20},{16,8},{20,12},{24,0},{28,4},{1,25},{... | collective-permute-start | bytes 442376 | tf_op jit(solution)/shard_map/ppermute | solution.py:22
  394.4 15.2 %collective-permute-start.61 = (bf16[96,768]{1,0:T(8,128)(2,1)S(1)}, bf16[96,768]{1,0:T(8,128)(2,1)S(1)}, u32[]{:S(2)}, u32[]{:S(2)}) collective-permute-start(bf16[96,768]{1,0:T(8,128)(2,1)S(1)} %get-tuple-element.56), channel_id=1, source_target_pairs={{0,8},{4,12},{8,0},{12,4},{16,24},{20,28},{24,16},{28,20},{1,9},{5... | collective-permute-start | bytes 442376 | tf_op jit(solution)/shard_map/ppermute | solution.py:22
  394.5 18.4 %collective-permute-start.62 = (bf16[96,768]{1,0:T(8,128)(2,1)S(1)}, bf16[96,768]{1,0:T(8,128)(2,1)S(1)}, u32[]{:S(2)}, u32[]{:S(2)}) collective-permute-start(bf16[96,768]{1,0:T(8,128)(2,1)S(1)} %get-tuple-element.58), channel_id=1, source_target_pairs={{0,16},{4,20},{8,24},{12,28},{16,0},{20,4},{24,8},{28,12},{1,17},{... | collective-permute-start | bytes 442376 | tf_op jit(solution)/shard_map/ppermute | solution.py:22
  395.8 17.1 %collective-permute-start.63 = (bf16[96,768]{1,0:T(8,128)(2,1)S(1)}, bf16[96,768]{1,0:T(8,128)(2,1)S(1)}, u32[]{:S(2)}, u32[]{:S(2)}) collective-permute-start(bf16[96,768]{1,0:T(8,128)(2,1)S(1)} %get-tuple-element.57), channel_id=1, source_target_pairs={{0,24},{4,28},{8,16},{12,20},{16,8},{20,12},{24,0},{28,4},{1,25},{... | collective-permute-start | bytes 442376 | tf_op jit(solution)/shard_map/ppermute | solution.py:22
  399.0 24.0 %collective-permute-start.53 = (bf16[96,768]{1,0:T(8,128)(2,1)S(1)}, bf16[96,768]{1,0:T(8,128)(2,1)S(1)}, u32[]{:S(2)}, u32[]{:S(2)}) collective-permute-start(bf16[96,768]{1,0:T(8,128)(2,1)S(1)} %add_convert_fusion.3), channel_id=1, source_target_pairs={{0,8},{4,12},{8,0},{12,4},{16,24},{20,28},{24,16},{28,20},{1,9},{5... | collective-permute-start | bytes 442376 | tf_op jit(solution)/shard_map/ppermute | solution.py:22
  409.6 16.7 %collective-permute-start.54 = (bf16[96,768]{1,0:T(8,128)(2,1)S(1)}, bf16[96,768]{1,0:T(8,128)(2,1)S(1)}, u32[]{:S(2)}, u32[]{:S(2)}) collective-permute-start(bf16[96,768]{1,0:T(8,128)(2,1)S(1)} %add_convert_fusion.3), channel_id=1, source_target_pairs={{0,16},{4,20},{8,24},{12,28},{16,0},{20,4},{24,8},{28,12},{1,17},{... | collective-permute-start | bytes 442376 | tf_op jit(solution)/shard_map/ppermute | solution.py:22
  409.6 19.7 %collective-permute-start.55 = (bf16[96,768]{1,0:T(8,128)(2,1)S(1)}, bf16[96,768]{1,0:T(8,128)(2,1)S(1)}, u32[]{:S(2)}, u32[]{:S(2)}) collective-permute-start(bf16[96,768]{1,0:T(8,128)(2,1)S(1)} %add_convert_fusion.3), channel_id=1, source_target_pairs={{0,24},{4,28},{8,16},{12,20},{16,8},{20,12},{24,0},{28,4},{1,25},{... | collective-permute-start | bytes 442376 | tf_op jit(solution)/shard_map/ppermute | solution.py:22
  412.9 17.3 %collective-permute-start.64 = (bf16[96,768]{1,0:T(8,128)(2,1)S(1)}, bf16[96,768]{1,0:T(8,128)(2,1)S(1)}, u32[]{:S(2)}, u32[]{:S(2)}) collective-permute-start(bf16[96,768]{1,0:T(8,128)(2,1)S(1)} %add_convert_fusion.2), channel_id=1, source_target_pairs={{0,8},{4,12},{8,0},{12,4},{16,24},{20,28},{24,16},{28,20},{1,9},{5... | collective-permute-start | bytes 442376 | tf_op jit(solution)/shard_map/ppermute | solution.py:22
  422.9 11.6 %collective-permute-start.65 = (bf16[96,768]{1,0:T(8,128)(2,1)S(1)}, bf16[96,768]{1,0:T(8,128)(2,1)S(1)}, u32[]{:S(2)}, u32[]{:S(2)}) collective-permute-start(bf16[96,768]{1,0:T(8,128)(2,1)S(1)} %add_convert_fusion.2), channel_id=1, source_target_pairs={{0,16},{4,20},{8,24},{12,28},{16,0},{20,4},{24,8},{28,12},{1,17},{... | collective-permute-start | bytes 442376 | tf_op jit(solution)/shard_map/ppermute | solution.py:22
  423.0 11.6 %collective-permute-start.66 = (bf16[96,768]{1,0:T(8,128)(2,1)S(1)}, bf16[96,768]{1,0:T(8,128)(2,1)S(1)}, u32[]{:S(2)}, u32[]{:S(2)}) collective-permute-start(bf16[96,768]{1,0:T(8,128)(2,1)S(1)} %add_convert_fusion.2), channel_id=1, source_target_pairs={{0,24},{4,28},{8,16},{12,20},{16,8},{20,12},{24,0},{28,4},{1,25},{... | collective-permute-start | bytes 442376 | tf_op jit(solution)/shard_map/ppermute | solution.py:22
  426.3 14.2 %collective-permute-start.45 = (bf16[96,768]{1,0:T(8,128)(2,1)S(1)}, bf16[96,768]{1,0:T(8,128)(2,1)S(1)}, u32[]{:S(2)}, u32[]{:S(2)}) collective-permute-start(bf16[96,768]{1,0:T(8,128)(2,1)S(1)} %copy-done.51), channel_id=1, source_target_pairs={{0,4},{4,0},{8,12},{12,8},{16,20},{20,16},{24,28},{28,24},{1,5},{5... | collective-permute-start | bytes 442376 | tf_op jit(solution)/shard_map/ppermute | solution.py:22
  429.3 13.0 %collective-permute-start.34 = (bf16[384,576]{1,0:T(8,128)(2,1)}, bf16[384,576]{1,0:T(8,128)(2,1)}, u32[]{:S(2)}, u32[]{:S(2)}) collective-permute-start(bf16[384,576]{1,0:T(8,128)(2,1)} %bitcast_select_fusion), channel_id=1, source_target_pairs={{0,4},{4,0},{8,12},{12,8},{16,20},{20,16},{24,28},{28,24},{1,5},{5... | collective-permute-start | bytes 1327112 | tf_op jit(solution)/shard_map/ppermute | solution.py:22
  435.7 19.0 %collective-permute-start.67 = (bf16[384,768]{1,0:T(8,128)(2,1)S(1)}, bf16[384,768]{1,0:T(8,128)(2,1)S(1)}, u32[]{:S(2)}, u32[]{:S(2)}) collective-permute-start(bf16[384,768]{1,0:T(8,128)(2,1)S(1)} %bitcast.254), channel_id=1, source_target_pairs={{0,4},{4,0},{8,12},{12,8},{16,20},{20,16},{24,28},{28,24},{1,5},{5... | collective-permute-start | bytes 1769480 | tf_op jit(solution)/shard_map/ppermute | solution.py:22
  439.3 24.5 %collective-permute-start.56 = (bf16[384,768]{1,0:T(8,128)(2,1)S(1)}, bf16[384,768]{1,0:T(8,128)(2,1)}, u32[]{:S(2)}, u32[]{:S(2)}) collective-permute-start(bf16[384,768]{1,0:T(8,128)(2,1)S(1)} %bitcast.252), channel_id=1, source_target_pairs={{0,4},{4,0},{8,12},{12,8},{16,20},{20,16},{24,28},{28,24},{1,5},{5... | collective-permute-start | bytes 1769480 | tf_op jit(solution)/shard_map/ppermute | solution.py:22
  (149 other events, 1054.7 us)
